TPU v7x, 512 devices: a whole 4x8x8 slice. The times are simulated.
512 devices in a mesh: pp: 16 (over z, core), ep: 32 (over x, y).
Axes of the slice: x: 4, y: 8, z: 8, core: 2. Of those that a mesh axis runs over, the one named last changes fastest.
Arguments:
- pending_activations: bfloat16 [16, 2048, 3584], P('pp', 'ep'), may hold values from -6 to 6
- incoming_microbatches: bfloat16 [1, 2048, 3584], P(None, 'ep'), may hold values from -6 to 6
- layer_rescale_factor: float32 [16, 3584], P('pp'), may hold values from 0.5 to 1.5
- gating_projection_matrix: bfloat16 [16, 3584, 4096], P('pp', None, 'ep'), may hold values from -0.09375 to 0.09375
- widening_projection_matrix: bfloat16 [16, 3584, 4096], P('pp', None, 'ep'), may hold values from -0.09375 to 0.09375
- output_projection_matrix: bfloat16 [16, 4096, 3584], P('pp', 'ep'), may hold values from -0.1875 to 0.1875
- picked_specialist_ids: int32 [2, 16, 2048, 1], P(None, 'pp', 'ep'), may hold values from 0 to 3; in each aligned block of 64 rows (0 to 63, 64 to 127, ..., all dimensions but the last counted through in order) at most 17 rows name the same one
- dispatcher_probability_values: float32 [2, 16, 2048, 1], P(None, 'pp', 'ep'), may hold values from 0.1 to 1
Outputs:
- section_outputs: bfloat16 [2, 16, 2048, 3584], P(None, 'pp', 'ep')
Inputs may be any that keep to these rules, and one draw needn't show every extreme that they name: `picked_specialist_ids`: each token names exactly one expert. In each step and section, the 64 rows of one device (aligned blocks of the token dimension) name each expert at most 17 times, a bound that some block reaches.
All inputs are finite; a program needn't handle non-finite values.
Results may differ from a plain program's by a relative error of at most 0.0055.
Values may be sent and summed in bfloat16 or wider, within the bound.
No kernel may reach another device: no remote copies, remote signals or barrier semaphores. Data moves between devices by JAX's collectives and lax.ppermute only.
A program may use at most 64 MiB of HBM per device.

v0:
```python
import jax
import jax.numpy as jnp
from jax import lax
from jax.sharding import PartitionSpec as P

GROUP = 8


def from_behind(value, axis, steps):
    count = lax.axis_size(axis)
    leading, last = (max(0, -steps), min(count, count - steps))
    return lax.ppermute(value, axis, [(source, source + steps) for source in range(leading, last)])


def section_layer(inputs, gain_row, gate_w, up_w, down_w, chosen, scores):
    row_count = inputs.shape[0]
    feat_width = inputs.shape[1]
    top_count = chosen.shape[1]
    owners = lax.axis_size("ep")
    experts = owners // GROUP
    slot_count = min(
        row_count,
        row_count * top_count // experts + max(1, row_count * top_count // (16 * experts)),
    )
    float_rows = inputs.astype(jnp.float32)
    variance = jnp.mean(float_rows * float_rows, axis=-1, keepdims=True)
    normed = (float_rows * lax.rsqrt(variance + 1e-06) * gain_row).astype(jnp.bfloat16)
    expert_grid = jnp.arange(experts, dtype=jnp.int32)
    hits = (chosen[:, :, None] == expert_grid[None, None, :]).astype(jnp.int32)
    flat_hits = hits.reshape(row_count * top_count, experts)
    before = jnp.cumsum(flat_hits, axis=0) - flat_hits
    slot_pos = jnp.sum(before * flat_hits, axis=1)
    slot_ids = chosen.reshape(-1) * slot_count + slot_pos
    slot_grid = jnp.arange(experts * slot_count, dtype=jnp.int32)
    picker = (slot_grid[:, None] == slot_ids[None, :]).astype(jnp.float32)
    picker = jnp.sum(picker.reshape(experts * slot_count, row_count, top_count), axis=2).astype(
        jnp.bfloat16
    )
    packed = jnp.dot(picker, normed, preferred_element_type=jnp.float32).astype(jnp.bfloat16)
    outgoing = jnp.broadcast_to(
        packed.reshape(experts, 1, slot_count, feat_width), (experts, GROUP, slot_count, feat_width)
    )
    outgoing = outgoing.reshape(owners, slot_count, feat_width)
    received = lax.all_to_all(outgoing, "ep", split_axis=0, concat_axis=0, tiled=True)
    sources = received.shape[0]
    items = received.shape[1]
    row_block = received.reshape(sources * items, received.shape[2])
    gate_val = jnp.dot(row_block, gate_w, preferred_element_type=jnp.float32)
    up_val = jnp.dot(row_block, up_w, preferred_element_type=jnp.float32)
    active = (jax.nn.silu(gate_val) * up_val).astype(jnp.bfloat16)
    result = jnp.dot(active, down_w, preferred_element_type=jnp.float32).astype(jnp.bfloat16)
    partials = result.reshape(sources, items, result.shape[1])
    returned = lax.all_to_all(partials, "ep", split_axis=0, concat_axis=0, tiled=True)
    summed = jnp.sum(
        returned.astype(jnp.float32).reshape(experts, GROUP, slot_count, feat_width), axis=1
    )
    summed = summed.reshape(experts * slot_count, feat_width)
    slot_table = slot_ids.reshape(row_count, top_count)
    mixing = jnp.sum(
        scores[:, :, None]
        * (slot_table[:, :, None] == slot_grid[None, None, :]).astype(jnp.float32),
        axis=1,
    )
    combined = jnp.dot(
        mixing, summed, precision=lax.Precision.HIGHEST, preferred_element_type=jnp.float32
    )
    return (float_rows + combined).astype(jnp.bfloat16)


def local(
    pending_activations,
    incoming_microbatches,
    layer_rescale_factor,
    gating_projection_matrix,
    widening_projection_matrix,
    output_projection_matrix,
    picked_specialist_ids,
    dispatcher_probability_values,
):
    tick_total = picked_specialist_ids.shape[0]
    first_section = lax.axis_index("pp") == 0
    present_activation_list = pending_activations[0]
    outputs = []
    for tick_index in range(tick_total):
        produced = section_layer(
            present_activation_list,
            layer_rescale_factor[0],
            gating_projection_matrix[0],
            widening_projection_matrix[0],
            output_projection_matrix[0],
            picked_specialist_ids[tick_index, 0],
            dispatcher_probability_values[tick_index, 0],
        )
        outputs.append(produced)
        if tick_index + 1 < tick_total:
            passed = from_behind(produced, "pp", 1)
            present_activation_list = jnp.where(
                first_section, incoming_microbatches[tick_index], passed
            )
    return jnp.stack(outputs)[:, None]


def solution(mesh):
    in_specs = (
        P("pp", "ep", None),
        P(None, "ep", None),
        P("pp", None),
        P("pp", None, "ep"),
        P("pp", None, "ep"),
        P("pp", "ep", None),
        P(None, "pp", "ep", None),
        P(None, "pp", "ep", None),
    )
    out_specs = P(None, "pp", "ep", None)
    return jax.shard_map(local, mesh=mesh, in_specs=in_specs, out_specs=out_specs, check_vma=False)
```

profile of v0, /device:TPU:249, one launch (start us, length us, event | category | flops | bytes accessed | tf_op | source)
XLA Modules:
  0.0 602.7 jit_solution(3124529134308731337)
XLA Ops:
  1.1 1.2 fusion.6
  4.0 1.4 convolution_convert_fusion.3
  5.9 129.9 %all_to_all.20 = bf16[32,17,3584]{2,1,0:T(8,128)(2,1)} all-to-all(bf16[32,17,3584]{2,1,0:T(8,128)(2,1)S(1)} %bitcast.68), channel_id=1, replica_groups=mesh['pp'=16,'ep'=32] {'ep'}, dimensions={0} | all-to-all | bytes 7798784 | tf_op jit(solution)/shard_map/all_to_all | solution.py:44
  135.8 5.6 reshape.326
  141.4 3.4 fusion.20
  144.8 8.2 %convolution_convert_fusion.1 = bf16[544,3584]{1,0:T(8,128)(2,1)} fusion(bf16[544,3584]{1,0:T(8,128)(2,1)} %reshape.326, bf16[1,128,3584]{2,1,0:T(8,128)(2,1)S(1)} %copy-done, bf16[1,3584,128]{2,1,0:T(8,128)(2,1)S(1)} %copy-done.2, f32[544,128]{1,0:T(8,128)S(1)} %fusion.20), kind=kOutput, calls=%fused_computation.3 | convolution fusion | flops 1000611840 | bytes 9912320 | tf_op jit(solution)/shard_map/dot_general | solution.py:51
  153.0 5.5 reshape.327
  158.5 8.1 %all-to-all-start.1 = ((bf16[32,17,3584]{2,1,0:T(8,128)(2,1)}), bf16[32,17,3584]{2,1,0:T(8,128)(2,1)}, u32[]{:S(2)}, u32[]{:S(2)}) async-start(bf16[32,17,3584]{2,1,0:T(8,128)(2,1)} %reshape.327), calls=%async_computation.1 | async-start | bytes 11010048 | tf_op jit(solution)/shard_map/all_to_all | solution.py:53
  166.9 123.9 %all-to-all-done.1 = bf16[32,17,3584]{2,1,0:T(8,128)(2,1)} async-done(((bf16[32,17,3584]{2,1,0:T(8,128)(2,1)}), bf16[32,17,3584]{2,1,0:T(8,128)(2,1)}, u32[]{:S(2)}, u32[]{:S(2)}) %all-to-all-start.1) | async-done | bytes 3899424 | tf_op jit(solution)/shard_map/all_to_all | solution.py:53
  290.7 3.6 convert_reduce_fusion.1
  294.5 1.9 fusion
  296.4 5.6 collective-permute-start
  302.0 5.4 collective-permute-done
  307.4 1.3 fusion.9
  310.4 129.5 %all_to_all.21 = bf16[32,17,3584]{2,1,0:T(8,128)(2,1)} all-to-all(bf16[32,17,3584]{2,1,0:T(8,128)(2,1)S(1)} %bitcast.69), channel_id=1, replica_groups=mesh['pp'=16,'ep'=32] {'ep'}, dimensions={0} | all-to-all | bytes 7798784 | tf_op jit(solution)/shard_map/all_to_all | solution.py:44
  439.9 5.6 reshape.332
  445.5 3.3 fusion.18
  448.9 8.2 %convolution_convert_fusion = bf16[544,3584]{1,0:T(8,128)(2,1)} fusion(bf16[544,3584]{1,0:T(8,128)(2,1)} %reshape.332, bf16[1,128,3584]{2,1,0:T(8,128)(2,1)S(1)} %copy-done, bf16[1,3584,128]{2,1,0:T(8,128)(2,1)S(1)} %copy-done.3, f32[544,128]{1,0:T(8,128)S(1)} %fusion.18), kind=kOutput, calls=%fused_computation.2 | convolution fusion | flops 1000611840 | bytes 9912320 | tf_op jit(solution)/shard_map/dot_general | solution.py:51
  457.1 5.6 reshape.333
  462.7 7.1 %all-to-all-start.3 = ((bf16[32,17,3584]{2,1,0:T(8,128)(2,1)}), bf16[32,17,3584]{2,1,0:T(8,128)(2,1)}, u32[]{:S(2)}, u32[]{:S(2)}) async-start(bf16[32,17,3584]{2,1,0:T(8,128)(2,1)} %reshape.333), calls=%async_computation.3 | async-start | bytes 11010048 | tf_op jit(solution)/shard_map/all_to_all | solution.py:53
  470.0 125.0 %all-to-all-done.3 = bf16[32,17,3584]{2,1,0:T(8,128)(2,1)} async-done(((bf16[32,17,3584]{2,1,0:T(8,128)(2,1)}), bf16[32,17,3584]{2,1,0:T(8,128)(2,1)}, u32[]{:S(2)}, u32[]{:S(2)}) %all-to-all-start.3) | async-done | bytes 3899424 | tf_op jit(solution)/shard_map/all_to_all | solution.py:53
  595.0 3.6 convert_reduce_fusion
  598.7 1.9 fusion.2
  600.6 2.0 maximum_bitcast_fusion
  (36 shorter events, 5.6 us)
Async XLA Ops:
  0.0 144.8 %copy-start = (bf16[1,128,3584]{2,1,0:T(8,128)(2,1)S(1)}, bf16[1,128,3584]{2,1,0:T(8,128)(2,1)}, u32[]{:S(2)}) copy-start(bf16[1,128,3584]{2,1,0:T(8,128)(2,1)} %param.13) | copy-start | bytes 2752516
  135.8 5.6 copy-start.6
  141.4 3.4 copy-start.2
  158.5 8.2 %copy-start.5 = (f32[2,1,64,1]{2,3,1,0:T(1,128)S(1)}, f32[2,1,64,1]{2,3,1,0:T(1,128)}, u32[]{:S(2)}) copy-start(f32[2,1,64,1]{2,3,1,0:T(1,128)} %param.15) | copy-start | bytes 1540
  158.5 132.2 %all-to-all-start.1 = ((bf16[32,17,3584]{2,1,0:T(8,128)(2,1)}), bf16[32,17,3584]{2,1,0:T(8,128)(2,1)}, u32[]{:S(2)}, u32[]{:S(2)}) async-start(bf16[32,17,3584]{2,1,0:T(8,128)(2,1)} %reshape.327), calls=%async_computation.1 | async-start | bytes 11010048 | tf_op jit(solution)/shard_map/all_to_all | solution.py:53
  296.4 12.3 %copy-start.4 = (bf16[64,3584]{1,0:T(8,128)(2,1)}, bf16[64,3584]{1,0:T(8,128)(2,1)S(1)}, u32[]{:S(2)}) copy-start(bf16[64,3584]{1,0:T(8,128)(2,1)S(1)} %fusion) | copy-start | bytes 1376260
  296.4 11.0 %collective-permute-start = (bf16[64,3584]{1,0:T(8,128)(2,1)S(1)}, bf16[64,3584]{1,0:T(8,128)(2,1)S(1)}, u32[]{:S(2)}, u32[]{:S(2)}) collective-permute-start(bf16[64,3584]{1,0:T(8,128)(2,1)S(1)} %fusion), channel_id=1, source_target_pairs={{0,32},{32,64},{64,96},{96,128},{128,160},{160,192},{192,224},{224... | collective-permute-start | bytes 1376264 | tf_op jit(solution)/shard_map/ppermute | solution.py:12
  308.7 0.8 copy-start.1
  439.9 5.6 copy-start.7
  445.5 3.4 copy-start.3
  462.7 132.3 %all-to-all-start.3 = ((bf16[32,17,3584]{2,1,0:T(8,128)(2,1)}), bf16[32,17,3584]{2,1,0:T(8,128)(2,1)}, u32[]{:S(2)}, u32[]{:S(2)}) async-start(bf16[32,17,3584]{2,1,0:T(8,128)(2,1)} %reshape.333), calls=%async_computation.3 | async-start | bytes 11010048 | tf_op jit(solution)/shard_map/all_to_all | solution.py:53
where the time goes:
time: 604 us; the launch traced here: 603 us
  blocking collectives  259 us (43%)
  waiting for transfers between devices  254 us (42%)
  matrix products  28.7 us (5%)
  local copies, waits for them, and re-layouts  25.3 us (4%)
  starting transfers between devices  20.9 us (3%)
  other arithmetic  14 us (2%)
    all_to_all x2, blocking collectives, section_layer(): lax.all_to_all(outgoing, 'ep', split_axis=0, concat_axis=0, tiled=True)  259 us
    all_to_all x2, waiting for transfers between devices, section_layer(): lax.all_to_all(partials, 'ep', split_axis=0, concat_axis=0, tiled=True)  249 us
    dot_general x2, matrix products, section_layer(): jnp.dot(active, down_w, preferred_element_type=jnp.float32)  16.4 us
    all_to_all x2, starting transfers between devices, section_layer(): lax.all_to_all(partials, 'ep', split_axis=0, concat_axis=0, tiled=True)  15.3 us
  transfers between devices with their start and end apart: 3, of which 3 were waited for; matrix products, arithmetic and copies ran while one was open for 0% of the time, Pallas kernels for 0%

commit v1 on v0

v1 whole, which is shorter than its diff:
```python
import jax
import jax.numpy as jnp
from jax import lax
from jax.sharding import Mesh, PartitionSpec as P

GROUP = 8


def slots_of(chosen, slot_count, experts):
    hits = (chosen[:, None] == jnp.arange(experts, dtype=jnp.int32)[None, :]).astype(jnp.int32)
    before = jnp.cumsum(hits, axis=0) - hits
    return chosen * slot_count + jnp.sum(before * hits, axis=1)


def section_layer(inputs, gain_row, gate_w, up_w, down_w, chosen, scores):
    row_count, width = inputs.shape
    experts = lax.axis_size("x")
    ring = lax.axis_size("y")
    slot_count = 17
    float_rows = inputs.astype(jnp.float32)
    variance = jnp.mean(float_rows * float_rows, axis=-1, keepdims=True)
    normed = (float_rows * lax.rsqrt(variance + 1e-06) * gain_row).astype(jnp.bfloat16)
    slot_ids = slots_of(chosen[:, 0], slot_count, experts)
    slot_grid = jnp.arange(experts * slot_count, dtype=jnp.int32)
    picker = (slot_grid[:, None] == slot_ids[None, :]).astype(jnp.bfloat16)
    packed = jnp.dot(picker, normed, preferred_element_type=jnp.float32).astype(jnp.bfloat16)
    sent = packed.reshape(experts, slot_count, width)
    mine = lax.all_to_all(sent, "x", split_axis=0, concat_axis=0, tiled=True)
    mine = mine.reshape(experts * slot_count, width)
    held = experts * slot_count
    padded = -(-held // 8) * 8
    mine = jnp.pad(mine, ((0, padded - held), (0, 0)))
    rows = lax.all_gather(mine, "y", axis=0, tiled=True)
    gate_val = jnp.dot(rows, gate_w, preferred_element_type=jnp.float32)
    up_val = jnp.dot(rows, up_w, preferred_element_type=jnp.float32)
    active = (jax.nn.silu(gate_val) * up_val).astype(jnp.bfloat16)
    partial = jnp.dot(active, down_w, preferred_element_type=jnp.float32).astype(jnp.bfloat16)
    summed = lax.psum_scatter(partial, "y", scatter_dimension=0, tiled=True)
    back = summed[:held].reshape(experts, slot_count, width)
    back = lax.all_to_all(back, "x", split_axis=0, concat_axis=0, tiled=True)
    back = back.reshape(held, width)
    unpick = (slot_ids[:, None] == slot_grid[None, :]).astype(jnp.bfloat16)
    combined = scores * jnp.dot(unpick, back, preferred_element_type=jnp.float32)
    return (float_rows + combined).astype(jnp.bfloat16)


def local(pending, incoming, gain, gate_w, up_w, down_w, chosen, scores):
    tick_total = chosen.shape[0]
    first_section = lax.axis_index("pp") == 0
    count = lax.axis_size("pp")
    rows = pending[0]
    outputs = []
    for tick in range(tick_total):
        produced = section_layer(
            rows, gain[0], gate_w[0], up_w[0], down_w[0], chosen[tick, 0], scores[tick, 0]
        )
        outputs.append(produced)
        if tick + 1 < tick_total:
            passed = lax.ppermute(produced, "pp", [(i, i + 1) for i in range(count - 1)])
            rows = jnp.where(first_section, incoming[tick], passed)
    return jnp.stack(outputs)[:, None]


def solution(mesh):
    fine = Mesh(mesh.devices.reshape(mesh.shape["pp"], -1, GROUP), ("pp", "x", "y"))
    ep = ("x", "y")
    in_specs = (
        P("pp", ep, None),
        P(None, ep, None),
        P("pp", None),
        P("pp", None, ep),
        P("pp", None, ep),
        P("pp", ep, None),
        P(None, "pp", ep, None),
        P(None, "pp", ep, None),
    )
    out_specs = P(None, "pp", ep, None)
    return jax.shard_map(local, mesh=fine, in_specs=in_specs, out_specs=out_specs, check_vma=False)
```

time: 604 us -> 348 us (0.58)
  the two profiles are of different devices: /device:TPU:249 before, /device:TPU:24 now
where the time goes in v1:
time: 348 us
  waiting for transfers between devices  246 us (71%)
  blocking collectives  42.6 us (12%)
  matrix products  26.7 us (8%)
  between operations  13.3 us (4%)
  local copies, waits for them, and re-layouts  7.68 us (2%)
  starting transfers between devices  5.65 us (2%)
  other arithmetic  5.54 us (2%)
    all_gather x2, waiting for transfers between devices, section_layer(): rows = lax.all_gather(mine, 'y', axis=0, tiled=True)  121 us
    reduce_scatter x2, waiting for transfers between devices, section_layer(): summed = lax.psum_scatter(partial, 'y', scatter_dimension=0, tiled=True)  113 us
    all_to_all x2, blocking collectives, section_layer(): mine = lax.all_to_all(sent, 'x', split_axis=0, concat_axis=0, tiled=True)  27.4 us
    dot_general x2, matrix products, section_layer(): jnp.dot(active, down_w, preferred_element_type=jnp.float32)  17 us
    all_to_all x1, blocking collectives, section_layer(): back = lax.all_to_all(back, 'x', split_axis=0, concat_axis=0, tiled=True)  15.2 us
    all_to_all x1, waiting for transfers between devices, section_layer(): back = lax.all_to_all(back, 'x', split_axis=0, concat_axis=0, tiled=True)  11.1 us
    dot_general x2, matrix products, section_layer(): gate_val = jnp.dot(rows, gate_w, preferred_element_type=jnp.float32)  7.29 us
  transfers between devices with their start and end apart: 6, of which 6 were waited for; matrix products, arithmetic and copies ran while one was open for 0% of the time, Pallas kernels for 0%

profile of v1, /device:TPU:24, one launch (start us, length us, event | category | flops | bytes accessed | tf_op | source)
XLA Modules:
  0.0 347.5 jit_solution(16498930131038805519)
XLA Ops:
  6.5 1.3 fusion.10
  10.5 1.4 convolution_convert_fusion.3
  12.0 15.3 %all_to_all.20 = bf16[4,17,3584]{2,1,0:T(8,128)(2,1)S(1)} all-to-all(bf16[4,17,3584]{2,1,0:T(8,128)(2,1)S(1)} %reshape.78), channel_id=1, replica_groups=mesh['pp'=16,'x'=4,'y'=8] {'x'}, dimensions={0} | all-to-all | bytes 974848 | tf_op jit(solution)/shard_map/all_to_all | solution.py:28
  27.5 0.8 pad.7
  28.4 58.9 %all-gather.3.cloned.1.call-done = bf16[576,3584]{1,0:T(8,128)(2,1)} async-done(((bf16[72,3584]{1,0:T(8,128)(2,1)}), bf16[576,3584]{1,0:T(8,128)(2,1)}) %all-gather.3.cloned.1.call-update) | async-done | bytes 4128784 | tf_op jit(solution)/shard_map/all_gather | solution.py:33
  87.4 3.6 %fusion.21 = f32[576,128]{1,0:T(8,128)S(1)} fusion(bf16[576,3584]{1,0:T(8,128)(2,1)} %all-gather.3.cloned.1.call-done, bf16[1,3584,128]{2,1,0:T(8,128)(2,1)} %param.11), kind=kOutput, calls=%fused_computation.32 | convolution fusion | flops 528482304 | bytes 5341184 | tf_op jit(solution)/shard_map/dot_general | solution.py:34
  91.0 8.5 %convolution_convert_fusion.1 = bf16[576,3584]{1,0:T(8,128)(2,1)} fusion(bf16[576,3584]{1,0:T(8,128)(2,1)} %all-gather.3.cloned.1.call-done, bf16[1,128,3584]{2,1,0:T(8,128)(2,1)S(1)} %copy-done, bf16[1,3584,128]{2,1,0:T(8,128)(2,1)S(1)} %copy-done.2, f32[576,128]{1,0:T(8,128)S(1)} %fusion.21), kind=kOutput, calls=%fused_computation.1 | convolution fusion | flops 1059471360 | bytes 10387456 | tf_op jit(solution)/shard_map/dot_general | solution.py:37
  99.5 56.3 %reduce-scatter.3.cloned.1.call-done = bf16[72,3584]{1,0:T(8,128)(2,1)} async-done(((bf16[576,3584]{1,0:T(8,128)(2,1)}), bf16[72,3584]{1,0:T(8,128)(2,1)}) %reduce-scatter.3.cloned.1.call-update) | async-done | bytes 516112 | tf_op jit(solution)/shard_map/reduce_scatter | solution.py:38
  155.8 2.0 reshape.80
  157.9 4.2 %all-to-all-start.1 = ((bf16[4,17,3584]{2,1,0:T(8,128)(2,1)}), bf16[4,17,3584]{2,1,0:T(8,128)(2,1)S(1)}, u32[]{:S(2)}, u32[]{:S(2)}) async-start(bf16[4,17,3584]{2,1,0:T(8,128)(2,1)} %reshape.80), calls=%async_computation.2 | async-start | bytes 1376256 | tf_op jit(solution)/shard_map/all_to_all | solution.py:40
  162.1 11.1 %all-to-all-done.1 = bf16[4,17,3584]{2,1,0:T(8,128)(2,1)S(1)} async-done(((bf16[4,17,3584]{2,1,0:T(8,128)(2,1)}), bf16[4,17,3584]{2,1,0:T(8,128)(2,1)S(1)}, u32[]{:S(2)}, u32[]{:S(2)}) %all-to-all-start.1) | async-done | bytes 487456 | tf_op jit(solution)/shard_map/all_to_all | solution.py:40
  173.8 1.3 collective-permute-start
  175.1 1.4 collective-permute-done
  176.5 1.3 fusion.7
  178.3 12.1 %all_to_all.21 = bf16[4,17,3584]{2,1,0:T(8,128)(2,1)} all-to-all(bf16[4,17,3584]{2,1,0:T(8,128)(2,1)S(1)} %reshape.82), channel_id=1, replica_groups=mesh['pp'=16,'x'=4,'y'=8] {'x'}, dimensions={0} | all-to-all | bytes 974848 | tf_op jit(solution)/shard_map/all_to_all | solution.py:28
  190.4 1.3 reshape.83
  191.7 0.8 pad.8
  192.6 62.1 %all-gather.5.cloned.1.call-done = bf16[576,3584]{1,0:T(8,128)(2,1)} async-done(((bf16[72,3584]{1,0:T(8,128)(2,1)}), bf16[576,3584]{1,0:T(8,128)(2,1)}) %all-gather.5.cloned.1.call-update) | async-done | bytes 4128784 | tf_op jit(solution)/shard_map/all_gather | solution.py:33
  254.6 3.6 %fusion.19 = f32[576,128]{1,0:T(8,128)S(1)} fusion(bf16[576,3584]{1,0:T(8,128)(2,1)} %all-gather.5.cloned.1.call-done, bf16[1,3584,128]{2,1,0:T(8,128)(2,1)} %param.11), kind=kOutput, calls=%fused_computation.30 | convolution fusion | flops 528482304 | bytes 5341184 | tf_op jit(solution)/shard_map/dot_general | solution.py:34
  258.3 8.5 %convolution_convert_fusion = bf16[576,3584]{1,0:T(8,128)(2,1)} fusion(bf16[576,3584]{1,0:T(8,128)(2,1)} %all-gather.5.cloned.1.call-done, bf16[1,128,3584]{2,1,0:T(8,128)(2,1)S(1)} %copy-done, bf16[1,3584,128]{2,1,0:T(8,128)(2,1)S(1)} %copy-done.2, f32[576,128]{1,0:T(8,128)S(1)} %fusion.19), kind=kOutput, calls=%fused_computation | convolution fusion | flops 1059471360 | bytes 10387456 | tf_op jit(solution)/shard_map/dot_general | solution.py:37
  266.8 56.3 %reduce-scatter.5.cloned.1.call-done = bf16[72,3584]{1,0:T(8,128)(2,1)} async-done(((bf16[576,3584]{1,0:T(8,128)(2,1)}), bf16[72,3584]{1,0:T(8,128)(2,1)}) %reduce-scatter.5.cloned.1.call-update) | async-done | bytes 516112 | tf_op jit(solution)/shard_map/reduce_scatter | solution.py:38
  323.1 1.2 reshape.84
  324.3 15.2 %all_to_all.22 = bf16[4,17,3584]{2,1,0:T(8,128)(2,1)S(1)} all-to-all(bf16[4,17,3584]{2,1,0:T(8,128)(2,1)S(1)} %reshape.84), channel_id=1, replica_groups=mesh['pp'=16,'x'=4,'y'=8] {'x'}, dimensions={0} | all-to-all | bytes 974848 | tf_op jit(solution)/shard_map/all_to_all | solution.py:40
  340.0 1.0 maximum_bitcast_fusion
  (39 shorter events, 4.7 us)
Async XLA Ops:
  6.5 84.5 %copy-start = (bf16[1,128,3584]{2,1,0:T(8,128)(2,1)S(1)}, bf16[1,128,3584]{2,1,0:T(8,128)(2,1)}, u32[]{:S(2)}) copy-start(bf16[1,128,3584]{2,1,0:T(8,128)(2,1)} %param.13) | copy-start | bytes 2752516
  6.5 80.8 %all-gather.3.cloned.1.call-start = ((), (), s32[]{:S(2)}) async-start(), calls=%async_computation.6 | async-start | bytes 4644864 | tf_op jit(solution)/shard_map/all_gather | solution.py:33
  27.5 63.5 %copy-start.2 = (bf16[1,3584,128]{2,1,0:T(8,128)(2,1)S(1)}, bf16[1,3584,128]{2,1,0:T(8,128)(2,1)}, u32[]{:S(2)}) copy-start(bf16[1,3584,128]{2,1,0:T(8,128)(2,1)} %param.12) | copy-start | bytes 2752516
  28.4 127.4 %reduce-scatter.3.cloned.1.call-start = ((), (), s32[]{:S(2)}) async-start(), calls=%async_computation.7 | async-start | bytes 4644864 | tf_op jit(solution)/shard_map/reduce_scatter | solution.py:38
  99.5 62.6 %copy-start.5 = (f32[2,1,64,1]{2,3,1,0:T(1,128)S(1)}, f32[2,1,64,1]{2,3,1,0:T(1,128)}, u32[]{:S(2)}) copy-start(f32[2,1,64,1]{2,3,1,0:T(1,128)} %param.15) | copy-start | bytes 1540
  99.5 73.9 %copy-start.1 = (bf16[1,64,3584]{2,1,0:T(8,128)(2,1)S(1)}, bf16[1,64,3584]{2,1,0:T(8,128)(2,1)}, u32[]{:S(2)}) copy-start(bf16[1,64,3584]{2,1,0:T(8,128)(2,1)} %param.8) | copy-start | bytes 1376260
  157.9 15.4 %all-to-all-start.1 = ((bf16[4,17,3584]{2,1,0:T(8,128)(2,1)}), bf16[4,17,3584]{2,1,0:T(8,128)(2,1)S(1)}, u32[]{:S(2)}, u32[]{:S(2)}) async-start(bf16[4,17,3584]{2,1,0:T(8,128)(2,1)} %reshape.80), calls=%async_computation.2 | async-start | bytes 1376256 | tf_op jit(solution)/shard_map/all_to_all | solution.py:40
  162.1 92.5 %all-gather.5.cloned.1.call-start = ((), (), s32[]{:S(2)}) async-start(), calls=%async_computation.8 | async-start | bytes 4644864 | tf_op jit(solution)/shard_map/all_gather | solution.py:33
  173.8 4.0 %copy-start.3 = (bf16[64,3584]{1,0:T(8,128)(2,1)}, bf16[64,3584]{1,0:T(8,128)(2,1)S(1)}, u32[]{:S(2)}) copy-start(bf16[64,3584]{1,0:T(8,128)(2,1)S(1)} %fusion.3) | copy-start | bytes 1376260
  173.8 2.7 collective-permute-start
  192.5 130.5 %reduce-scatter.5.cloned.1.call-start = ((), (), s32[]{:S(2)}) async-start(), calls=%async_computation.9 | async-start | bytes 4644864 | tf_op jit(solution)/shard_map/reduce_scatter | solution.py:38
  266.8 73.2 %copy-start.4 = (bf16[64,3584]{1,0:T(8,128)(2,1)S(1)}, bf16[64,3584]{1,0:T(8,128)(2,1)}, u32[]{:S(2)}) copy-start(bf16[64,3584]{1,0:T(8,128)(2,1)} %copy-done.3) | copy-start | bytes 1376260
Sparse Core Ops, SparseCore 0:
  28.5 58.7 all-gather.2
  99.7 56.0 reduce-scatter.2
  192.6 61.9 all-gather.4
  266.9 56.0 reduce-scatter.4

commit v2 on v1

v2 whole, which is shorter than its diff:
```python
import jax
import jax.numpy as jnp
from jax import lax
from jax.experimental import pallas as pl
from jax.experimental.pallas import tpu as pltpu
from jax.sharding import Mesh, PartitionSpec as P

GROUP = 8
SLOTS = 17
SUM_ROWS = 71


def expert_kernel(rows_ref, gate_ref, up_ref, down_ref, out_ref, rows, both, active, packed):
    tall = rows_ref.shape[0] // GROUP
    short = out_ref.shape[0] // GROUP
    hidden = gate_ref.shape[1]
    rows[...] = rows_ref[...]
    both[:, :hidden] = gate_ref[...]
    both[:, hidden:] = up_ref[...]
    mixed = jnp.dot(rows[...], both[...], preferred_element_type=jnp.float32)
    gate_val, up_val = mixed[:, :hidden], mixed[:, hidden:]
    active[...] = gate_val / (1.0 + jnp.exp(-gate_val)) * up_val
    for i in range(GROUP):
        packed[i * short : (i + 1) * short, :] = active[i * tall : i * tall + short, :]
    acts = packed[...].astype(jnp.bfloat16)
    tile = down_ref.shape[1] // 4
    for j in range(4):
        cols = slice(j * tile, (j + 1) * tile)
        out_ref[:, cols] = jnp.dot(
            acts, down_ref[:, cols], preferred_element_type=jnp.float32
        ).astype(jnp.bfloat16)


def expert_parts(rows, gate_w, up_w, down_w):
    total, width = rows.shape
    hidden = gate_w.shape[1]
    return pl.pallas_call(
        expert_kernel,
        out_shape=jax.ShapeDtypeStruct((GROUP * SUM_ROWS, width), jnp.bfloat16),
        in_specs=[pl.BlockSpec(memory_space=pltpu.VMEM)] * 4,
        out_specs=pl.BlockSpec(memory_space=pltpu.VMEM),
        scratch_shapes=[
            pltpu.VMEM((total, width), jnp.bfloat16),
            pltpu.VMEM((width, 2 * hidden), jnp.bfloat16),
            pltpu.VMEM((total, hidden), jnp.float32),
            pltpu.VMEM((GROUP * SUM_ROWS, hidden), jnp.float32),
        ],
        compiler_params=pltpu.CompilerParams(vmem_limit_bytes=32 * 2**20),
        cost_estimate=pl.CostEstimate(
            flops=6 * total * width * hidden,
            bytes_accessed=4 * total * width + 6 * width * hidden,
            transcendentals=total * hidden,
        ),
    )(rows, gate_w, up_w, down_w)


def wide(value):
    return value.astype(jnp.float32)


def exchange(packed):
    experts = lax.axis_size("x")
    blocks = packed.reshape(experts, SLOTS, packed.shape[1])
    moved = lax.all_to_all(blocks, "x", split_axis=0, concat_axis=0, tiled=True)
    return moved.reshape(packed.shape)


def experts_of(packed, gate_w, up_w, down_w):
    held = packed.shape[0]
    tall = -(-held // 8) * 8
    mine = jnp.pad(exchange(packed), ((0, tall - held), (0, 0)))
    rows = lax.all_gather(mine.astype(jnp.float16), "y", axis=0, tiled=True)
    parts = expert_parts(rows.astype(jnp.bfloat16), gate_w, up_w, down_w)
    summed = lax.psum_scatter(parts, "y", scatter_dimension=0, tiled=True)
    summed = lax.optimization_barrier(summed)
    return exchange(summed[:held])


def section_layer(inputs, gain_row, gate_w, up_w, down_w, chosen, scores):
    experts = lax.axis_size("x")
    float_rows = wide(inputs)
    variance = jnp.mean(float_rows * float_rows, axis=-1, keepdims=True)
    normed = (float_rows * lax.rsqrt(variance + 1e-06) * gain_row).astype(jnp.bfloat16)
    chosen = chosen[:, 0]
    hits = (chosen[:, None] == jnp.arange(experts, dtype=jnp.int32)[None, :]).astype(jnp.int32)
    place = jnp.sum((jnp.cumsum(hits, axis=0) - hits) * hits, axis=1)
    slot = chosen * SLOTS + place

    count = experts * SLOTS
    pick = (jnp.arange(count, dtype=jnp.int32)[:, None] == slot[None, :]).astype(jnp.bfloat16)
    packed = jnp.dot(pick, normed, preferred_element_type=jnp.float32).astype(jnp.bfloat16)
    back = experts_of(packed, gate_w, up_w, down_w)
    combined = jnp.dot(pick.T, back, preferred_element_type=jnp.float32)
    return (float_rows + scores * combined).astype(jnp.bfloat16)


def local(pending, incoming, gain, gate_w, up_w, down_w, chosen, scores):
    tick_total = chosen.shape[0]
    first_section = lax.axis_index("pp") == 0
    count = lax.axis_size("pp")
    rows = pending[0]
    outputs = []
    for tick in range(tick_total):
        produced = section_layer(
            rows, gain[0], gate_w[0], up_w[0], down_w[0], chosen[tick, 0], scores[tick, 0]
        )
        outputs.append(produced)
        if tick + 1 < tick_total:
            passed = lax.ppermute(produced, "pp", [(i, i + 1) for i in range(count - 1)])
            rows = jnp.where(first_section, incoming[tick], passed)
    return jnp.stack(outputs)[:, None]


def solution(mesh):
    fine = Mesh(mesh.devices.reshape(mesh.shape["pp"], -1, GROUP), ("pp", "x", "y"))
    ep = ("x", "y")
    in_specs = (
        P("pp", ep, None),
        P(None, ep, None),
        P("pp", None),
        P("pp", None, ep),
        P("pp", None, ep),
        P("pp", ep, None),
        P(None, "pp", ep, None),
        P(None, "pp", ep, None),
    )
    out_specs = P(None, "pp", ep, None)
    return jax.shard_map(local, mesh=fine, in_specs=in_specs, out_specs=out_specs, check_vma=False)
```

time: 348 us -> 315 us (0.905)
  the two profiles are of different devices: /device:TPU:24 before, /device:TPU:224 now
where the time goes in v2:
time: 315 us; the launch traced here: 314 us
  blocking collectives  228 us (72%)
  local copies, waits for them, and re-layouts  25.8 us (8%)
  waiting for transfers between devices  24.9 us (8%)
  starting transfers between devices  11 us (3%)
  Pallas kernels  9.29 us (3%)
  other arithmetic  9.1 us (3%)
  matrix products  5.04 us (2%)
    unnamed x2, blocking collectives  99.3 us
    all_gather x2, blocking collectives, experts_of(): rows = lax.all_gather(mine.astype(jnp.float16), 'y', axis=0, tiled=True)  85 us
    all_to_all x3, blocking collectives, exchange(): moved = lax.all_to_all(blocks, 'x', split_axis=0, concat_axis=0, tiled=True)  43.3 us
    unnamed x21, local copies, waits for them, and re-layouts  16.2 us
    pallas_call x2, Pallas kernels, expert_parts(): pl.pallas_call(expert_kernel, out_shape=jax.ShapeDtypeStruct((GROUP * SUM...  9.29 us
    all_to_all x1, waiting for transfers between devices, exchange(): moved = lax.all_to_all(blocks, 'x', split_axis=0, concat_axis=0, tiled=True)  9 us
    ppermute x1, waiting for transfers between devices, local(): lax.ppermute(produced, 'pp', [(i, i + 1) for i in range(count - 1)])  8.18 us
    unnamed x2, waiting for transfers between devices  7.7 us
  transfers between devices with their start and end apart: 4, of which 4 were waited for; matrix products, arithmetic and copies ran while one was open for 0% of the time, Pallas kernels for 0%

profile of v2, /device:TPU:224, one launch (start us, length us, event | category | flops | bytes accessed | tf_op | source)
XLA Modules:
  0.0 313.5 jit_solution(2861267134812640883)
XLA Ops:
  5.4 15.3 %all_to_all.20 = bf16[4,17,3584]{2,1,0:T(8,128)(2,1)S(1)} all-to-all(bf16[4,17,3584]{2,1,0:T(8,128)(2,1)S(1)} %reshape.62), channel_id=1, replica_groups=mesh['pp'=16,'x'=4,'y'=8] {'x'}, dimensions={0} | all-to-all | bytes 974848 | tf_op jit(solution)/shard_map/all_to_all | solution.py:64
  21.0 41.6 %all-gather.2 = f16[576,3584]{1,0:T(8,128)(2,1)S(1)} all-gather(f16[72,3584]{1,0:T(8,128)(2,1)S(1)} %pad_convert_fusion.1), channel_id=1, replica_groups=mesh['pp'=16,'x'=4,'y'=8] {'y'}, dimensions={0}, use_global_device_ids=true | all-gather | bytes 4644864 | tf_op jit(solution)/shard_map/all_gather | solution.py:72
  64.3 4.6 %shard_map.82 = bf16[568,3584]{1,0:T(8,128)(2,1)S(1)} custom-call(bf16[576,3584]{1,0:T(8,128)(2,1)S(1)} %convert_element_type.56.rows_ref, bf16[3584,128]{1,0:T(8,128)(2,1)S(1)} %bitcast.42, bf16[3584,128]{1,0:T(8,128)(2,1)S(1)} %bitcast.44, bf16[128,3584]{1,0:T(8,128)(2,1)S(1)} %bitcast.46), custom_call_target="tpu_custom_call" | custom-call | flops 1585446912 | bytes 11010048 | tf_op jit(solution)/shard_map/pallas_call | solution.py:37
  70.9 49.4 %fusion = bf16[72,3584]{1,0:T(8,128)(2,1)} fusion(bf16[568,3584]{1,0:T(8,128)(2,1)} %copy-done), kind=kCustom, calls=%all-reduce-scatter | all-reduce-scatter fusion | flops 2064385 | bytes 4589568
  121.2 2.5 collective-permute-start.1
  125.6 2.9 collective-permute-done.1
  128.4 4.9 %concatenate = bf16[79,3584]{1,0:T(8,128)(2,1)} concatenate(bf16[7,3584]{1,0:T(8,128)(2,1)S(1)} %collective-permute-done.1, bf16[72,3584]{1,0:T(8,128)(2,1)} %fusion), dimensions={0} | concatenate | bytes 1132544
  135.3 2.0 reshape.64
  137.4 4.2 %all-to-all-start.1 = ((bf16[4,17,3584]{2,1,0:T(8,128)(2,1)}), bf16[4,17,3584]{2,1,0:T(8,128)(2,1)}, u32[]{:S(2)}, u32[]{:S(2)}) async-start(bf16[4,17,3584]{2,1,0:T(8,128)(2,1)} %reshape.64), calls=%async_computation.1 | async-start | bytes 1376256 | tf_op jit(solution)/shard_map/all_to_all | solution.py:64
  141.6 9.0 %all-to-all-done.1 = bf16[4,17,3584]{2,1,0:T(8,128)(2,1)} async-done(((bf16[4,17,3584]{2,1,0:T(8,128)(2,1)}), bf16[4,17,3584]{2,1,0:T(8,128)(2,1)}, u32[]{:S(2)}, u32[]{:S(2)}) %all-to-all-start.1) | async-done | bytes 487456 | tf_op jit(solution)/shard_map/all_to_all | solution.py:64
  150.6 2.0 reshape.65
  152.6 2.1 fusion.4
  156.7 8.2 %collective-permute-done = bf16[64,3584]{1,0:T(8,128)(2,1)} collective-permute-done((bf16[64,3584]{1,0:T(8,128)(2,1)}, bf16[64,3584]{1,0:T(8,128)(2,1)}, u32[]{:S(2)}, u32[]{:S(2)}) %collective-permute-start) | collective-permute-done | bytes 458784 | tf_op jit(solution)/shard_map/ppermute | solution.py:109
  167.5 2.0 reshape.66
  169.5 16.6 %all_to_all.21 = bf16[4,17,3584]{2,1,0:T(8,128)(2,1)} all-to-all(bf16[4,17,3584]{2,1,0:T(8,128)(2,1)} %reshape.66), channel_id=1, replica_groups=mesh['pp'=16,'x'=4,'y'=8] {'x'}, dimensions={0} | all-to-all | bytes 974848 | tf_op jit(solution)/shard_map/all_to_all | solution.py:64
  186.1 2.0 reshape.67
  189.3 43.5 %all-gather.3 = f16[576,3584]{1,0:T(8,128)(2,1)S(1)} all-gather(f16[72,3584]{1,0:T(8,128)(2,1)S(1)} %pad_convert_fusion), channel_id=1, replica_groups=mesh['pp'=16,'x'=4,'y'=8] {'y'}, dimensions={0}, use_global_device_ids=true | all-gather | bytes 4644864 | tf_op jit(solution)/shard_map/all_gather | solution.py:72
  233.4 4.6 %shard_map.83 = bf16[568,3584]{1,0:T(8,128)(2,1)S(1)} custom-call(bf16[576,3584]{1,0:T(8,128)(2,1)S(1)} %convert_element_type.63.rows_ref, bf16[3584,128]{1,0:T(8,128)(2,1)S(1)} %bitcast.43, bf16[3584,128]{1,0:T(8,128)(2,1)S(1)} %bitcast.45, bf16[128,3584]{1,0:T(8,128)(2,1)S(1)} %bitcast.47), custom_call_target="tpu_custom_call" | custom-call | flops 1585446912 | bytes 11010048 | tf_op jit(solution)/shard_map/pallas_call | solution.py:37
  239.9 49.9 %fusion.1 = bf16[72,3584]{1,0:T(8,128)(2,1)S(1)} fusion(bf16[568,3584]{1,0:T(8,128)(2,1)} %copy-done.1), kind=kCustom, calls=%all-reduce-scatter.1 | all-reduce-scatter fusion | flops 2064385 | bytes 4589568
  289.9 2.5 collective-permute-start.2
  292.3 4.8 %collective-permute-done.2 = bf16[7,3584]{1,0:T(8,128)(2,1)S(1)} collective-permute-done((bf16[7,3584]{1,0:T(8,128)(2,1)S(1)}, bf16[7,3584]{1,0:T(8,128)(2,1)S(1)}, u32[]{:S(2)}, u32[]{:S(2)}) %collective-permute-start.2) | collective-permute-done | bytes 50208
  297.2 2.2 concatenate.1
  299.6 11.3 %all_to_all.22 = bf16[4,17,3584]{2,1,0:T(8,128)(2,1)S(1)} all-to-all(bf16[4,17,3584]{2,1,0:T(8,128)(2,1)S(1)} %reshape.68), channel_id=1, replica_groups=mesh['pp'=16,'x'=4,'y'=8] {'x'}, dimensions={0} | all-to-all | bytes 974848 | tf_op jit(solution)/shard_map/all_to_all | solution.py:64
  311.5 2.0 maximum_bitcast_fusion
  (44 shorter events, 22.4 us)
Async XLA Ops:
  62.6 1.2 copy-start.2
  62.6 1.5 copy-start.3
  62.6 1.7 copy-start.4
  69.0 1.9 copy-start
  70.9 70.7 %copy-start.6 = (f32[2,1,64,1]{2,3,1,0:T(1,128)S(1)}, f32[2,1,64,1]{2,3,1,0:T(1,128)}, u32[]{:S(2)}) copy-start(f32[2,1,64,1]{2,3,1,0:T(1,128)} %param.15) | copy-start | bytes 1540
  120.3 32.3 %copy-start.5 = (bf16[1,64,3584]{2,1,0:T(8,128)(2,1)S(1)}, bf16[1,64,3584]{2,1,0:T(8,128)(2,1)}, u32[]{:S(2)}) copy-start(bf16[1,64,3584]{2,1,0:T(8,128)(2,1)} %param.8) | copy-start | bytes 1376260
  121.2 7.3 %collective-permute-start.1 = (bf16[7,3584]{1,0:T(8,128)(2,1)S(1)}, bf16[7,3584]{1,0:T(8,128)(2,1)S(1)}, u32[]{:S(2)}, u32[]{:S(2)}) collective-permute-start(bf16[7,3584]{1,0:T(8,128)(2,1)S(1)} %slice.26), channel_id=1, source_target_pairs={{0,1},{1,2},{2,3},{3,4},{4,5},{5,6},{6,7},{8,9},{9,10},{10,11},{11... | collective-permute-start | bytes 150536
  137.4 13.2 %all-to-all-start.1 = ((bf16[4,17,3584]{2,1,0:T(8,128)(2,1)}), bf16[4,17,3584]{2,1,0:T(8,128)(2,1)}, u32[]{:S(2)}, u32[]{:S(2)}) async-start(bf16[4,17,3584]{2,1,0:T(8,128)(2,1)} %reshape.64), calls=%async_computation.1 | async-start | bytes 1376256 | tf_op jit(solution)/shard_map/all_to_all | solution.py:64
  154.8 10.1 %collective-permute-start = (bf16[64,3584]{1,0:T(8,128)(2,1)}, bf16[64,3584]{1,0:T(8,128)(2,1)}, u32[]{:S(2)}, u32[]{:S(2)}) collective-permute-start(bf16[64,3584]{1,0:T(8,128)(2,1)} %fusion.4), channel_id=1, source_target_pairs={{0,32},{32,64},{64,96},{96,128},{128,160},{160,192},{192,224},{224... | collective-permute-start | bytes 1376264 | tf_op jit(solution)/shard_map/ppermute | solution.py:109
  238.0 1.9 copy-start.1
  289.9 7.3 %collective-permute-start.2 = (bf16[7,3584]{1,0:T(8,128)(2,1)S(1)}, bf16[7,3584]{1,0:T(8,128)(2,1)S(1)}, u32[]{:S(2)}, u32[]{:S(2)}) collective-permute-start(bf16[7,3584]{1,0:T(8,128)(2,1)S(1)} %slice.27), channel_id=1, source_target_pairs={{0,1},{1,2},{2,3},{3,4},{4,5},{5,6},{6,7},{8,9},{9,10},{10,11},{11... | collective-permute-start | bytes 150536

commit v3 on v2

--- a/solution.py
+++ b/solution.py
@@ -7,73 +7,108 @@
 
 GROUP = 8
 SLOTS = 17
-SUM_ROWS = 71
+LANES = 24
 
 
-def expert_kernel(rows_ref, gate_ref, up_ref, down_ref, out_ref, rows, both, active, packed):
+def shift(value, steps):
+    size = lax.axis_size("y")
+    return lax.ppermute(value, "y", [(i, (i + steps) % size) for i in range(size)])
+
+
+def expert_kernel(me_ref, rows_ref, gate_ref, up_ref, down_ref, *refs):
+    outs, (both, active, turned) = refs[:-3], refs[-3:]
     tall = rows_ref.shape[0] // GROUP
-    short = out_ref.shape[0] // GROUP
-    hidden = gate_ref.shape[1]
-    rows[...] = rows_ref[...]
+    width, hidden = gate_ref.shape
     both[:, :hidden] = gate_ref[...]
     both[:, hidden:] = up_ref[...]
-    mixed = jnp.dot(rows[...], both[...], preferred_element_type=jnp.float32)
+    mixed = jnp.dot(rows_ref[...], both[...], preferred_element_type=jnp.float32)
     gate_val, up_val = mixed[:, :hidden], mixed[:, hidden:]
     active[...] = gate_val / (1.0 + jnp.exp(-gate_val)) * up_val
-    for i in range(GROUP):
-        packed[i * short : (i + 1) * short, :] = active[i * tall : i * tall + short, :]
-    acts = packed[...].astype(jnp.bfloat16)
-    tile = down_ref.shape[1] // 4
+    for d in range(GROUP):
+        owner = lax.rem(me_ref[0] + d, GROUP)
+        block = active[pl.ds(pl.multiple_of(owner * tall, 8), tall), :]
+        turned[d * tall : (d + 1) * tall, :] = block
+    acts = turned[...].astype(jnp.bfloat16)
+    tile = width // 4
     for j in range(4):
-        cols = slice(j * tile, (j + 1) * tile)
-        out_ref[:, cols] = jnp.dot(
-            acts, down_ref[:, cols], preferred_element_type=jnp.float32
+        part = jnp.dot(
+            acts, down_ref[:, j * tile : (j + 1) * tile], preferred_element_type=jnp.float32
         ).astype(jnp.bfloat16)
+        cols = slice((j % 2) * tile, (j % 2 + 1) * tile)
+        for d in range(GROUP):
+            outs[2 * d + j // 2][:, cols] = part[d * tall : (d + 1) * tall]
 
 
 def expert_parts(rows, gate_w, up_w, down_w):
     total, width = rows.shape
     hidden = gate_w.shape[1]
-    return pl.pallas_call(
+    me = lax.axis_index("y").astype(jnp.int32).reshape(1)
+    outs = pl.pallas_call(
         expert_kernel,
-        out_shape=jax.ShapeDtypeStruct((GROUP * SUM_ROWS, width), jnp.bfloat16),
-        in_specs=[pl.BlockSpec(memory_space=pltpu.VMEM)] * 4,
-        out_specs=pl.BlockSpec(memory_space=pltpu.VMEM),
+        out_shape=[pltpu.VMEM((total // GROUP, width // 2), jnp.bfloat16)] * (2 * GROUP),
+        in_specs=[pl.BlockSpec(memory_space=pltpu.SMEM)]
+        + [pl.BlockSpec(memory_space=pltpu.VMEM)] * 4,
+        out_specs=[pl.BlockSpec(memory_space=pltpu.VMEM)] * (2 * GROUP),
         scratch_shapes=[
-            pltpu.VMEM((total, width), jnp.bfloat16),
             pltpu.VMEM((width, 2 * hidden), jnp.bfloat16),
             pltpu.VMEM((total, hidden), jnp.float32),
-            pltpu.VMEM((GROUP * SUM_ROWS, hidden), jnp.float32),
+            pltpu.VMEM((total, hidden), jnp.float32),
         ],
-        compiler_params=pltpu.CompilerParams(vmem_limit_bytes=32 * 2**20),
+        compiler_params=pltpu.CompilerParams(vmem_limit_bytes=24 * 2**20),
         cost_estimate=pl.CostEstimate(
             flops=6 * total * width * hidden,
             bytes_accessed=4 * total * width + 6 * width * hidden,
             transcendentals=total * hidden,
         ),
-    )(rows, gate_w, up_w, down_w)
+    )(me, rows, gate_w, up_w, down_w)
+    return [(outs[2 * d], outs[2 * d + 1]) for d in range(GROUP)]
 
 
 def wide(value):
     return value.astype(jnp.float32)
 
 
+def plus(a, b):
+    return (a.astype(jnp.float32) + b.astype(jnp.float32)).astype(jnp.bfloat16)
+
+
 def exchange(packed):
     experts = lax.axis_size("x")
-    blocks = packed.reshape(experts, SLOTS, packed.shape[1])
+    blocks = packed.reshape(experts, LANES, packed.shape[1])
     moved = lax.all_to_all(blocks, "x", split_axis=0, concat_axis=0, tiled=True)
     return moved.reshape(packed.shape)
 
 
+def ring_sum(parts):
+    right_a, left_b = shift(parts[4][0], 1), shift(parts[4][1], -1)
+    right_b, left_a = shift(parts[3][1], 1), shift(parts[5][0], -1)
+    for s in (3, 2, 1):
+        right_a = shift(plus(right_a, parts[s][0]), 1)
+        left_b = shift(plus(left_b, parts[GROUP - s][1]), -1)
+        if s < 3:
+            right_b = shift(plus(right_b, parts[s][1]), 1)
+            left_a = shift(plus(left_a, parts[GROUP - s][0]), -1)
+    first = wide(parts[0][0]) + wide(right_a) + wide(left_a)
+    second = wide(parts[0][1]) + wide(right_b) + wide(left_b)
+    return first.astype(jnp.bfloat16), second.astype(jnp.bfloat16)
+
+
+def select(matrix, values):
+    return jnp.dot(matrix, values, preferred_element_type=jnp.float32).astype(jnp.bfloat16)
+
+
 def experts_of(packed, gate_w, up_w, down_w):
-    held = packed.shape[0]
+    experts = lax.axis_size("x")
+    held = experts * SLOTS
     tall = -(-held // 8) * 8
-    mine = jnp.pad(exchange(packed), ((0, tall - held), (0, 0)))
+    lane = jnp.arange(experts * LANES, dtype=jnp.int32)
+    dense = jnp.where(lane % LANES < SLOTS, lane // LANES * SLOTS + lane % LANES, -1)
+    spread = (dense[:, None] == jnp.arange(tall, dtype=jnp.int32)[None, :]).astype(jnp.bfloat16)
+    mine = select(spread.T, exchange(packed))
     rows = lax.all_gather(mine.astype(jnp.float16), "y", axis=0, tiled=True)
     parts = expert_parts(rows.astype(jnp.bfloat16), gate_w, up_w, down_w)
-    summed = lax.psum_scatter(parts, "y", scatter_dimension=0, tiled=True)
-    summed = lax.optimization_barrier(summed)
-    return exchange(summed[:held])
+    halves = [select(spread, half) for half in ring_sum(parts)]
+    return exchange(jnp.concatenate(halves, axis=1))
 
 
 def section_layer(inputs, gain_row, gate_w, up_w, down_w, chosen, scores):
@@ -84,9 +119,9 @@
     chosen = chosen[:, 0]
     hits = (chosen[:, None] == jnp.arange(experts, dtype=jnp.int32)[None, :]).astype(jnp.int32)
     place = jnp.sum((jnp.cumsum(hits, axis=0) - hits) * hits, axis=1)
-    slot = chosen * SLOTS + place
+    slot = chosen * LANES + place
 
-    count = experts * SLOTS
+    count = experts * LANES
     pick = (jnp.arange(count, dtype=jnp.int32)[:, None] == slot[None, :]).astype(jnp.bfloat16)
     packed = jnp.dot(pick, normed, preferred_element_type=jnp.float32).astype(jnp.bfloat16)
     back = experts_of(packed, gate_w, up_w, down_w)

time: 315 us -> 296 us (0.940)
  the two profiles are of different devices: /device:TPU:224 before, /device:TPU:344 now
where the time goes in v3:
time: 296 us; the launch traced here: 295 us
  blocking collectives  110 us (37%)
  starting transfers between devices  106 us (36%)
  waiting for transfers between devices  49 us (17%)
  other arithmetic  10.1 us (3%)
  Pallas kernels  9.48 us (3%)
  matrix products  7.28 us (2%)
    ppermute x28, starting transfers between devices, shift(): lax.ppermute(value, 'y', [(i, (i + steps) % size) for i in range(size)])  95.9 us
    all_gather x2, blocking collectives, experts_of(): rows = lax.all_gather(mine.astype(jnp.float16), 'y', axis=0, tiled=True)  85.3 us
    all_to_all x2, blocking collectives, exchange(): moved = lax.all_to_all(blocks, 'x', split_axis=0, concat_axis=0, tiled=True)  24.7 us
    ppermute x28, waiting for transfers between devices, shift(): lax.ppermute(value, 'y', [(i, (i + steps) % size) for i in range(size)])  20.7 us
    all_to_all x2, waiting for transfers between devices, exchange(): moved = lax.all_to_all(blocks, 'x', split_axis=0, concat_axis=0, tiled=True)  20.2 us
    pallas_call x2, Pallas kernels, expert_parts(): pl.pallas_call(expert_kernel, out_shape=[pltpu.VMEM((total // GROUP, widt...  9.48 us
    all_to_all x2, starting transfers between devices, exchange(): moved = lax.all_to_all(blocks, 'x', split_axis=0, concat_axis=0, tiled=True)  8.46 us
    ppermute x1, waiting for transfers between devices, local(): lax.ppermute(produced, 'pp', [(i, i + 1) for i in range(count - 1)])  8.07 us
  transfers between devices with their start and end apart: 31, of which 7 were waited for; matrix products, arithmetic and copies ran while one was open for 1% of the time, Pallas kernels for 0%

profile of v3, /device:TPU:344, one launch (start us, length us, event | category | flops | bytes accessed | tf_op | source)
XLA Modules:
  0.0 294.6 jit_solution(10284867853010669093)
XLA Ops:
  6.1 4.3 %all-to-all-start = ((bf16[4,24,3584]{2,1,0:T(8,128)(2,1)}), bf16[4,24,3584]{2,1,0:T(8,128)(2,1)S(1)}, u32[]{:S(2)}, u32[]{:S(2)}) async-start(bf16[4,24,3584]{2,1,0:T(8,128)(2,1)} %bitcast.5), calls=%async_computation | async-start | bytes 1376256 | tf_op jit(solution)/shard_map/all_to_all | solution.py:78
  10.5 11.2 %all-to-all-done = bf16[4,24,3584]{2,1,0:T(8,128)(2,1)S(1)} async-done(((bf16[4,24,3584]{2,1,0:T(8,128)(2,1)}), bf16[4,24,3584]{2,1,0:T(8,128)(2,1)S(1)}, u32[]{:S(2)}, u32[]{:S(2)}) %all-to-all-start) | async-done | bytes 688160 | tf_op jit(solution)/shard_map/all_to_all | solution.py:78
  22.1 43.6 %all-gather.2 = f16[576,3584]{1,0:T(8,128)(2,1)S(1)} all-gather(f16[72,3584]{1,0:T(8,128)(2,1)S(1)} %fusion.4), channel_id=1, replica_groups=mesh['pp'=16,'x'=4,'y'=8] {'y'}, dimensions={0}, use_global_device_ids=true | all-gather | bytes 4644864 | tf_op jit(solution)/shard_map/all_gather | solution.py:108
  67.4 4.7 %shard_map.82 = (bf16[72,1792]{1,0:T(8,128)(2,1)S(1)}, bf16[72,1792]{1,0:T(8,128)(2,1)S(1)}, bf16[72,1792]{1,0:T(8,128)(2,1)S(1)}, bf16[72,1792]{1,0:T(8,128)(2,...) custom-call(s32[1]{0:T(128)} %bitcast.3.me_ref, ...), custom_call_target="tpu_custom_call" | custom-call | flops 1585446912 | bytes 11010048 | tf_op jit(solution)/shard_map/pallas_call | solution.py:46
  84.2 5.1 %collective-permute-start.1 = (bf16[72,1792]{1,0:T(8,128)(2,1)S(1)}, bf16[72,1792]{1,0:T(8,128)(2,1)S(1)}, u32[]{:S(2)}, u32[]{:S(2)}) collective-permute-start(bf16[72,1792]{1,0:T(8,128)(2,1)S(1)} %add_convert_fusion.23), channel_id=1, source_target_pairs={{0,1},{1,2},{2,3},{3,4},{4,5},{5,6},{6,7},{7,0},{8,9},{9,10},{10,1... | collective-permute-start | bytes 774152 | tf_op jit(solution)/shard_map/ppermute | solution.py:15
  91.5 5.1 %collective-permute-start.8 = (bf16[72,1792]{1,0:T(8,128)(2,1)S(1)}, bf16[72,1792]{1,0:T(8,128)(2,1)S(1)}, u32[]{:S(2)}, u32[]{:S(2)}) collective-permute-start(bf16[72,1792]{1,0:T(8,128)(2,1)S(1)} %add_convert_fusion.17), channel_id=1, source_target_pairs={{0,1},{1,2},{2,3},{3,4},{4,5},{5,6},{6,7},{7,0},{8,9},{9,10},{10,1... | collective-permute-start | bytes 774152 | tf_op jit(solution)/shard_map/ppermute | solution.py:15
  98.7 5.1 %collective-permute-start.2 = (bf16[72,1792]{1,0:T(8,128)(2,1)S(1)}, bf16[72,1792]{1,0:T(8,128)(2,1)S(1)}, u32[]{:S(2)}, u32[]{:S(2)}) collective-permute-start(bf16[72,1792]{1,0:T(8,128)(2,1)S(1)} %add_convert_fusion.22), channel_id=1, source_target_pairs={{0,1},{1,2},{2,3},{3,4},{4,5},{5,6},{6,7},{7,0},{8,9},{9,10},{10,1... | collective-permute-start | bytes 774152 | tf_op jit(solution)/shard_map/ppermute | solution.py:15
  105.9 5.1 %collective-permute-start.9 = (bf16[72,1792]{1,0:T(8,128)(2,1)S(1)}, bf16[72,1792]{1,0:T(8,128)(2,1)S(1)}, u32[]{:S(2)}, u32[]{:S(2)}) collective-permute-start(bf16[72,1792]{1,0:T(8,128)(2,1)S(1)} %add_convert_fusion.16), channel_id=1, source_target_pairs={{0,1},{1,2},{2,3},{3,4},{4,5},{5,6},{6,7},{7,0},{8,9},{9,10},{10,1... | collective-permute-start | bytes 774152 | tf_op jit(solution)/shard_map/ppermute | solution.py:15
  113.2 5.1 %collective-permute-start.3 = (bf16[72,1792]{1,0:T(8,128)(2,1)S(1)}, bf16[72,1792]{1,0:T(8,128)(2,1)S(1)}, u32[]{:S(2)}, u32[]{:S(2)}) collective-permute-start(bf16[72,1792]{1,0:T(8,128)(2,1)S(1)} %add_convert_fusion.21), channel_id=1, source_target_pairs={{0,1},{1,2},{2,3},{3,4},{4,5},{5,6},{6,7},{7,0},{8,9},{9,10},{10,1... | collective-permute-start | bytes 774152 | tf_op jit(solution)/shard_map/ppermute | solution.py:15
  122.9 7.2 %collective-permute-done.13 = bf16[72,1792]{1,0:T(8,128)(2,1)S(1)} collective-permute-done((bf16[72,1792]{1,0:T(8,128)(2,1)S(1)}, bf16[72,1792]{1,0:T(8,128)(2,1)S(1)}, u32[]{:S(2)}, u32[]{:S(2)}) %collective-permute-start.13) | collective-permute-done | bytes 258080 | tf_op jit(solution)/shard_map/ppermute | solution.py:15
  135.5 9.0 %all-to-all-done.1 = bf16[4,24,3584]{2,1,0:T(8,128)(2,1)} async-done(((bf16[4,24,3584]{2,1,0:T(8,128)(2,1)}), bf16[4,24,3584]{2,1,0:T(8,128)(2,1)}, u32[]{:S(2)}, u32[]{:S(2)}) %all-to-all-start.1) | async-done | bytes 688160 | tf_op jit(solution)/shard_map/all_to_all | solution.py:78
  148.7 8.1 %collective-permute-done.14 = bf16[64,3584]{1,0:T(8,128)(2,1)S(1)} collective-permute-done((bf16[64,3584]{1,0:T(8,128)(2,1)}, bf16[64,3584]{1,0:T(8,128)(2,1)S(1)}, u32[]{:S(2)}, u32[]{:S(2)}) %collective-permute-start.14) | collective-permute-done | bytes 458784 | tf_op jit(solution)/shard_map/ppermute | solution.py:144
  158.5 13.3 %all_to_all.20 = bf16[4,24,3584]{2,1,0:T(8,128)(2,1)S(1)} all-to-all(bf16[4,24,3584]{2,1,0:T(8,128)(2,1)S(1)} %bitcast.55), channel_id=1, replica_groups=mesh['pp'=16,'x'=4,'y'=8] {'x'}, dimensions={0} | all-to-all | bytes 1376256 | tf_op jit(solution)/shard_map/all_to_all | solution.py:78
  172.1 41.7 %all-gather.3 = f16[576,3584]{1,0:T(8,128)(2,1)S(1)} all-gather(f16[72,3584]{1,0:T(8,128)(2,1)S(1)} %fusion.5), channel_id=1, replica_groups=mesh['pp'=16,'x'=4,'y'=8] {'y'}, dimensions={0}, use_global_device_ids=true | all-gather | bytes 4644864 | tf_op jit(solution)/shard_map/all_gather | solution.py:108
  214.4 4.7 %shard_map.83 = (bf16[72,1792]{1,0:T(8,128)(2,1)S(1)}, bf16[72,1792]{1,0:T(8,128)(2,1)S(1)}, bf16[72,1792]{1,0:T(8,128)(2,1)S(1)}, bf16[72,1792]{1,0:T(8,128)(2,...) custom-call(s32[1]{0:T(128)} %bitcast.3.me_ref, ...), custom_call_target="tpu_custom_call" | custom-call | flops 1585446912 | bytes 11010048 | tf_op jit(solution)/shard_map/pallas_call | solution.py:46
  219.2 4.5 %collective-permute-start.15 = (bf16[72,1792]{1,0:T(8,128)(2,1)S(1)}, bf16[72,1792]{1,0:T(8,128)(2,1)S(1)}, u32[]{:S(2)}, u32[]{:S(2)}) collective-permute-start(bf16[72,1792]{1,0:T(8,128)(2,1)S(1)} %get-tuple-element.54), channel_id=1, source_target_pairs={{0,1},{1,2},{2,3},{3,4},{4,5},{5,6},{6,7},{7,0},{8,9},{9,10},{10,1... | collective-permute-start | bytes 774152 | tf_op jit(solution)/shard_map/ppermute | solution.py:15
  225.6 5.1 %collective-permute-start.22 = (bf16[72,1792]{1,0:T(8,128)(2,1)S(1)}, bf16[72,1792]{1,0:T(8,128)(2,1)S(1)}, u32[]{:S(2)}, u32[]{:S(2)}) collective-permute-start(bf16[72,1792]{1,0:T(8,128)(2,1)S(1)} %get-tuple-element.62), channel_id=1, source_target_pairs={{0,1},{1,2},{2,3},{3,4},{4,5},{5,6},{6,7},{7,0},{8,9},{9,10},{10,1... | collective-permute-start | bytes 774152 | tf_op jit(solution)/shard_map/ppermute | solution.py:15
  232.8 5.1 %collective-permute-start.16 = (bf16[72,1792]{1,0:T(8,128)(2,1)S(1)}, bf16[72,1792]{1,0:T(8,128)(2,1)S(1)}, u32[]{:S(2)}, u32[]{:S(2)}) collective-permute-start(bf16[72,1792]{1,0:T(8,128)(2,1)S(1)} %add_convert_fusion.11), channel_id=1, source_target_pairs={{0,1},{1,2},{2,3},{3,4},{4,5},{5,6},{6,7},{7,0},{8,9},{9,10},{10,1... | collective-permute-start | bytes 774152 | tf_op jit(solution)/shard_map/ppermute | solution.py:15
  240.0 5.1 %collective-permute-start.23 = (bf16[72,1792]{1,0:T(8,128)(2,1)S(1)}, bf16[72,1792]{1,0:T(8,128)(2,1)S(1)}, u32[]{:S(2)}, u32[]{:S(2)}) collective-permute-start(bf16[72,1792]{1,0:T(8,128)(2,1)S(1)} %add_convert_fusion.5), channel_id=1, source_target_pairs={{0,1},{1,2},{2,3},{3,4},{4,5},{5,6},{6,7},{7,0},{8,9},{9,10},{10,1... | collective-permute-start | bytes 774152 | tf_op jit(solution)/shard_map/ppermute | solution.py:15
  247.2 5.1 %collective-permute-start.17 = (bf16[72,1792]{1,0:T(8,128)(2,1)S(1)}, bf16[72,1792]{1,0:T(8,128)(2,1)S(1)}, u32[]{:S(2)}, u32[]{:S(2)}) collective-permute-start(bf16[72,1792]{1,0:T(8,128)(2,1)S(1)} %add_convert_fusion.10), channel_id=1, source_target_pairs={{0,1},{1,2},{2,3},{3,4},{4,5},{5,6},{6,7},{7,0},{8,9},{9,10},{10,1... | collective-permute-start | bytes 774152 | tf_op jit(solution)/shard_map/ppermute | solution.py:15
  254.5 5.1 %collective-permute-start.24 = (bf16[72,1792]{1,0:T(8,128)(2,1)S(1)}, bf16[72,1792]{1,0:T(8,128)(2,1)S(1)}, u32[]{:S(2)}, u32[]{:S(2)}) collective-permute-start(bf16[72,1792]{1,0:T(8,128)(2,1)S(1)} %add_convert_fusion.4), channel_id=1, source_target_pairs={{0,1},{1,2},{2,3},{3,4},{4,5},{5,6},{6,7},{7,0},{8,9},{9,10},{10,1... | collective-permute-start | bytes 774152 | tf_op jit(solution)/shard_map/ppermute | solution.py:15
  261.7 5.1 %collective-permute-start.18 = (bf16[72,1792]{1,0:T(8,128)(2,1)S(1)}, bf16[72,1792]{1,0:T(8,128)(2,1)S(1)}, u32[]{:S(2)}, u32[]{:S(2)}) collective-permute-start(bf16[72,1792]{1,0:T(8,128)(2,1)S(1)} %add_convert_fusion.9), channel_id=1, source_target_pairs={{0,1},{1,2},{2,3},{3,4},{4,5},{5,6},{6,7},{7,0},{8,9},{9,10},{10,1... | collective-permute-start | bytes 774152 | tf_op jit(solution)/shard_map/ppermute | solution.py:15
  273.2 7.2 %collective-permute-done.28 = bf16[72,1792]{1,0:T(8,128)(2,1)S(1)} collective-permute-done((bf16[72,1792]{1,0:T(8,128)(2,1)S(1)}, bf16[72,1792]{1,0:T(8,128)(2,1)S(1)}, u32[]{:S(2)}, u32[]{:S(2)}) %collective-permute-start.28) | collective-permute-done | bytes 258080 | tf_op jit(solution)/shard_map/ppermute | solution.py:15
  280.8 11.4 %all_to_all.21 = bf16[4,24,3584]{2,1,0:T(8,128)(2,1)S(1)} all-to-all(bf16[4,24,3584]{2,1,0:T(8,128)(2,1)S(1)} %bitcast.56), channel_id=1, replica_groups=mesh['pp'=16,'x'=4,'y'=8] {'x'}, dimensions={0} | all-to-all | bytes 1376256 | tf_op jit(solution)/shard_map/all_to_all | solution.py:78
  (103 shorter events, 66.6 us)
Async XLA Ops:
  6.1 15.5 %all-to-all-start = ((bf16[4,24,3584]{2,1,0:T(8,128)(2,1)}), bf16[4,24,3584]{2,1,0:T(8,128)(2,1)S(1)}, u32[]{:S(2)}, u32[]{:S(2)}) async-start(bf16[4,24,3584]{2,1,0:T(8,128)(2,1)} %bitcast.5), calls=%async_computation | async-start | bytes 1376256 | tf_op jit(solution)/shard_map/all_to_all | solution.py:78
  72.2 12.0 %collective-permute-start = (bf16[72,1792]{1,0:T(8,128)(2,1)S(1)}, bf16[72,1792]{1,0:T(8,128)(2,1)S(1)}, u32[]{:S(2)}, u32[]{:S(2)}) collective-permute-start(bf16[72,1792]{1,0:T(8,128)(2,1)S(1)} %get-tuple-element.38), channel_id=1, source_target_pairs={{0,1},{1,2},{2,3},{3,4},{4,5},{5,6},{6,7},{7,0},{8,9},{9,10},{10,1... | collective-permute-start | bytes 774152 | tf_op jit(solution)/shard_map/ppermute | solution.py:15
  75.1 14.2 %collective-permute-start.4 = (bf16[72,1792]{1,0:T(8,128)(2,1)S(1)}, bf16[72,1792]{1,0:T(8,128)(2,1)S(1)}, u32[]{:S(2)}, u32[]{:S(2)}) collective-permute-start(bf16[72,1792]{1,0:T(8,128)(2,1)S(1)} %get-tuple-element.42), channel_id=1, source_target_pairs={{0,7},{1,0},{2,1},{3,2},{4,3},{5,4},{6,5},{7,6},{8,15},{9,8},{10,9... | collective-permute-start | bytes 774152 | tf_op jit(solution)/shard_map/ppermute | solution.py:15
  78.0 13.3 %collective-permute-start.7 = (bf16[72,1792]{1,0:T(8,128)(2,1)S(1)}, bf16[72,1792]{1,0:T(8,128)(2,1)S(1)}, u32[]{:S(2)}, u32[]{:S(2)}) collective-permute-start(bf16[72,1792]{1,0:T(8,128)(2,1)S(1)} %get-tuple-element.46), channel_id=1, source_target_pairs={{0,1},{1,2},{2,3},{3,4},{4,5},{5,6},{6,7},{7,0},{8,9},{9,10},{10,1... | collective-permute-start | bytes 774152 | tf_op jit(solution)/shard_map/ppermute | solution.py:15
  82.2 14.4 %collective-permute-start.10 = (bf16[72,1792]{1,0:T(8,128)(2,1)S(1)}, bf16[72,1792]{1,0:T(8,128)(2,1)S(1)}, u32[]{:S(2)}, u32[]{:S(2)}) collective-permute-start(bf16[72,1792]{1,0:T(8,128)(2,1)S(1)} %get-tuple-element.49), channel_id=1, source_target_pairs={{0,7},{1,0},{2,1},{3,2},{4,3},{5,4},{6,5},{7,6},{8,15},{9,8},{10,9... | collective-permute-start | bytes 774152 | tf_op jit(solution)/shard_map/ppermute | solution.py:15
  84.2 14.4 %collective-permute-start.1 = (bf16[72,1792]{1,0:T(8,128)(2,1)S(1)}, bf16[72,1792]{1,0:T(8,128)(2,1)S(1)}, u32[]{:S(2)}, u32[]{:S(2)}) collective-permute-start(bf16[72,1792]{1,0:T(8,128)(2,1)S(1)} %add_convert_fusion.23), channel_id=1, source_target_pairs={{0,1},{1,2},{2,3},{3,4},{4,5},{5,6},{6,7},{7,0},{8,9},{9,10},{10,1... | collective-permute-start | bytes 774152 | tf_op jit(solution)/shard_map/ppermute | solution.py:15
  89.4 14.4 %collective-permute-start.5 = (bf16[72,1792]{1,0:T(8,128)(2,1)S(1)}, bf16[72,1792]{1,0:T(8,128)(2,1)S(1)}, u32[]{:S(2)}, u32[]{:S(2)}) collective-permute-start(bf16[72,1792]{1,0:T(8,128)(2,1)S(1)} %add_convert_fusion.20), channel_id=1, source_target_pairs={{0,7},{1,0},{2,1},{3,2},{4,3},{5,4},{6,5},{7,6},{8,15},{9,8},{10,9... | collective-permute-start | bytes 774152 | tf_op jit(solution)/shard_map/ppermute | solution.py:15
  91.5 14.4 %collective-permute-start.8 = (bf16[72,1792]{1,0:T(8,128)(2,1)S(1)}, bf16[72,1792]{1,0:T(8,128)(2,1)S(1)}, u32[]{:S(2)}, u32[]{:S(2)}) collective-permute-start(bf16[72,1792]{1,0:T(8,128)(2,1)S(1)} %add_convert_fusion.17), channel_id=1, source_target_pairs={{0,1},{1,2},{2,3},{3,4},{4,5},{5,6},{6,7},{7,0},{8,9},{9,10},{10,1... | collective-permute-start | bytes 774152 | tf_op jit(solution)/shard_map/ppermute | solution.py:15
  96.7 14.4 %collective-permute-start.11 = (bf16[72,1792]{1,0:T(8,128)(2,1)S(1)}, bf16[72,1792]{1,0:T(8,128)(2,1)S(1)}, u32[]{:S(2)}, u32[]{:S(2)}) collective-permute-start(bf16[72,1792]{1,0:T(8,128)(2,1)S(1)} %add_convert_fusion.15), channel_id=1, source_target_pairs={{0,7},{1,0},{2,1},{3,2},{4,3},{5,4},{6,5},{7,6},{8,15},{9,8},{10,9... | collective-permute-start | bytes 774152 | tf_op jit(solution)/shard_map/ppermute | solution.py:15
  98.7 14.4 %collective-permute-start.2 = (bf16[72,1792]{1,0:T(8,128)(2,1)S(1)}, bf16[72,1792]{1,0:T(8,128)(2,1)S(1)}, u32[]{:S(2)}, u32[]{:S(2)}) collective-permute-start(bf16[72,1792]{1,0:T(8,128)(2,1)S(1)} %add_convert_fusion.22), channel_id=1, source_target_pairs={{0,1},{1,2},{2,3},{3,4},{4,5},{5,6},{6,7},{7,0},{8,9},{9,10},{10,1... | collective-permute-start | bytes 774152 | tf_op jit(solution)/shard_map/ppermute | solution.py:15
  103.9 18.7 %collective-permute-start.6 = (bf16[72,1792]{1,0:T(8,128)(2,1)S(1)}, bf16[72,1792]{1,0:T(8,128)(2,1)S(1)}, u32[]{:S(2)}, u32[]{:S(2)}) collective-permute-start(bf16[72,1792]{1,0:T(8,128)(2,1)S(1)} %add_convert_fusion.19), channel_id=1, source_target_pairs={{0,7},{1,0},{2,1},{3,2},{4,3},{5,4},{6,5},{7,6},{8,15},{9,8},{10,9... | collective-permute-start | bytes 774152 | tf_op jit(solution)/shard_map/ppermute | solution.py:15
  105.9 17.0 %collective-permute-start.9 = (bf16[72,1792]{1,0:T(8,128)(2,1)S(1)}, bf16[72,1792]{1,0:T(8,128)(2,1)S(1)}, u32[]{:S(2)}, u32[]{:S(2)}) collective-permute-start(bf16[72,1792]{1,0:T(8,128)(2,1)S(1)} %add_convert_fusion.16), channel_id=1, source_target_pairs={{0,1},{1,2},{2,3},{3,4},{4,5},{5,6},{6,7},{7,0},{8,9},{9,10},{10,1... | collective-permute-start | bytes 774152 | tf_op jit(solution)/shard_map/ppermute | solution.py:15
  131.3 13.2 %all-to-all-start.1 = ((bf16[4,24,3584]{2,1,0:T(8,128)(2,1)}), bf16[4,24,3584]{2,1,0:T(8,128)(2,1)}, u32[]{:S(2)}, u32[]{:S(2)}) async-start(bf16[4,24,3584]{2,1,0:T(8,128)(2,1)} %bitcast.53), calls=%async_computation.1 | async-start | bytes 1376256 | tf_op jit(solution)/shard_map/all_to_all | solution.py:78
  219.2 13.5 %collective-permute-start.15 = (bf16[72,1792]{1,0:T(8,128)(2,1)S(1)}, bf16[72,1792]{1,0:T(8,128)(2,1)S(1)}, u32[]{:S(2)}, u32[]{:S(2)}) collective-permute-start(bf16[72,1792]{1,0:T(8,128)(2,1)S(1)} %get-tuple-element.54), channel_id=1, source_target_pairs={{0,1},{1,2},{2,3},{3,4},{4,5},{5,6},{6,7},{7,0},{8,9},{9,10},{10,1... | collective-permute-start | bytes 774152 | tf_op jit(solution)/shard_map/ppermute | solution.py:15
  223.7 14.2 %collective-permute-start.19 = (bf16[72,1792]{1,0:T(8,128)(2,1)S(1)}, bf16[72,1792]{1,0:T(8,128)(2,1)S(1)}, u32[]{:S(2)}, u32[]{:S(2)}) collective-permute-start(bf16[72,1792]{1,0:T(8,128)(2,1)S(1)} %get-tuple-element.58), channel_id=1, source_target_pairs={{0,7},{1,0},{2,1},{3,2},{4,3},{5,4},{6,5},{7,6},{8,15},{9,8},{10,9... | collective-permute-start | bytes 774152 | tf_op jit(solution)/shard_map/ppermute | solution.py:15
  225.6 14.3 %collective-permute-start.22 = (bf16[72,1792]{1,0:T(8,128)(2,1)S(1)}, bf16[72,1792]{1,0:T(8,128)(2,1)S(1)}, u32[]{:S(2)}, u32[]{:S(2)}) collective-permute-start(bf16[72,1792]{1,0:T(8,128)(2,1)S(1)} %get-tuple-element.62), channel_id=1, source_target_pairs={{0,1},{1,2},{2,3},{3,4},{4,5},{5,6},{6,7},{7,0},{8,9},{9,10},{10,1... | collective-permute-start | bytes 774152 | tf_op jit(solution)/shard_map/ppermute | solution.py:15
  230.7 14.4 %collective-permute-start.25 = (bf16[72,1792]{1,0:T(8,128)(2,1)S(1)}, bf16[72,1792]{1,0:T(8,128)(2,1)S(1)}, u32[]{:S(2)}, u32[]{:S(2)}) collective-permute-start(bf16[72,1792]{1,0:T(8,128)(2,1)S(1)} %get-tuple-element.65), channel_id=1, source_target_pairs={{0,7},{1,0},{2,1},{3,2},{4,3},{5,4},{6,5},{7,6},{8,15},{9,8},{10,9... | collective-permute-start | bytes 774152 | tf_op jit(solution)/shard_map/ppermute | solution.py:15
  232.8 14.4 %collective-permute-start.16 = (bf16[72,1792]{1,0:T(8,128)(2,1)S(1)}, bf16[72,1792]{1,0:T(8,128)(2,1)S(1)}, u32[]{:S(2)}, u32[]{:S(2)}) collective-permute-start(bf16[72,1792]{1,0:T(8,128)(2,1)S(1)} %add_convert_fusion.11), channel_id=1, source_target_pairs={{0,1},{1,2},{2,3},{3,4},{4,5},{5,6},{6,7},{7,0},{8,9},{9,10},{10,1... | collective-permute-start | bytes 774152 | tf_op jit(solution)/shard_map/ppermute | solution.py:15
  238.0 14.4 %collective-permute-start.20 = (bf16[72,1792]{1,0:T(8,128)(2,1)S(1)}, bf16[72,1792]{1,0:T(8,128)(2,1)S(1)}, u32[]{:S(2)}, u32[]{:S(2)}) collective-permute-start(bf16[72,1792]{1,0:T(8,128)(2,1)S(1)} %add_convert_fusion.8), channel_id=1, source_target_pairs={{0,7},{1,0},{2,1},{3,2},{4,3},{5,4},{6,5},{7,6},{8,15},{9,8},{10,9... | collective-permute-start | bytes 774152 | tf_op jit(solution)/shard_map/ppermute | solution.py:15
  240.0 14.4 %collective-permute-start.23 = (bf16[72,1792]{1,0:T(8,128)(2,1)S(1)}, bf16[72,1792]{1,0:T(8,128)(2,1)S(1)}, u32[]{:S(2)}, u32[]{:S(2)}) collective-permute-start(bf16[72,1792]{1,0:T(8,128)(2,1)S(1)} %add_convert_fusion.5), channel_id=1, source_target_pairs={{0,1},{1,2},{2,3},{3,4},{4,5},{5,6},{6,7},{7,0},{8,9},{9,10},{10,1... | collective-permute-start | bytes 774152 | tf_op jit(solution)/shard_map/ppermute | solution.py:15
  245.2 14.4 %collective-permute-start.26 = (bf16[72,1792]{1,0:T(8,128)(2,1)S(1)}, bf16[72,1792]{1,0:T(8,128)(2,1)S(1)}, u32[]{:S(2)}, u32[]{:S(2)}) collective-permute-start(bf16[72,1792]{1,0:T(8,128)(2,1)S(1)} %add_convert_fusion.3), channel_id=1, source_target_pairs={{0,7},{1,0},{2,1},{3,2},{4,3},{5,4},{6,5},{7,6},{8,15},{9,8},{10,9... | collective-permute-start | bytes 774152 | tf_op jit(solution)/shard_map/ppermute | solution.py:15
  247.2 14.4 %collective-permute-start.17 = (bf16[72,1792]{1,0:T(8,128)(2,1)S(1)}, bf16[72,1792]{1,0:T(8,128)(2,1)S(1)}, u32[]{:S(2)}, u32[]{:S(2)}) collective-permute-start(bf16[72,1792]{1,0:T(8,128)(2,1)S(1)} %add_convert_fusion.10), channel_id=1, source_target_pairs={{0,1},{1,2},{2,3},{3,4},{4,5},{5,6},{6,7},{7,0},{8,9},{9,10},{10,1... | collective-permute-start | bytes 774152 | tf_op jit(solution)/shard_map/ppermute | solution.py:15
  252.5 20.4 %collective-permute-start.21 = (bf16[72,1792]{1,0:T(8,128)(2,1)S(1)}, bf16[72,1792]{1,0:T(8,128)(2,1)S(1)}, u32[]{:S(2)}, u32[]{:S(2)}) collective-permute-start(bf16[72,1792]{1,0:T(8,128)(2,1)S(1)} %add_convert_fusion.7), channel_id=1, source_target_pairs={{0,7},{1,0},{2,1},{3,2},{4,3},{5,4},{6,5},{7,6},{8,15},{9,8},{10,9... | collective-permute-start | bytes 774152 | tf_op jit(solution)/shard_map/ppermute | solution.py:15
  254.5 18.8 %collective-permute-start.24 = (bf16[72,1792]{1,0:T(8,128)(2,1)S(1)}, bf16[72,1792]{1,0:T(8,128)(2,1)S(1)}, u32[]{:S(2)}, u32[]{:S(2)}) collective-permute-start(bf16[72,1792]{1,0:T(8,128)(2,1)S(1)} %add_convert_fusion.4), channel_id=1, source_target_pairs={{0,1},{1,2},{2,3},{3,4},{4,5},{5,6},{6,7},{7,0},{8,9},{9,10},{10,1... | collective-permute-start | bytes 774152 | tf_op jit(solution)/shard_map/ppermute | solution.py:15
  (12 other events, 93.7 us)

commit v4 on v3

--- a/solution.py
+++ b/solution.py
@@ -111,36 +111,69 @@
     return exchange(jnp.concatenate(halves, axis=1))
 
 
-def section_layer(inputs, gain_row, gate_w, up_w, down_w, chosen, scores):
-    experts = lax.axis_size("x")
-    float_rows = wide(inputs)
+def normalise(rows, gain):
+    float_rows = wide(rows)
     variance = jnp.mean(float_rows * float_rows, axis=-1, keepdims=True)
-    normed = (float_rows * lax.rsqrt(variance + 1e-06) * gain_row).astype(jnp.bfloat16)
-    chosen = chosen[:, 0]
-    hits = (chosen[:, None] == jnp.arange(experts, dtype=jnp.int32)[None, :]).astype(jnp.int32)
-    place = jnp.sum((jnp.cumsum(hits, axis=0) - hits) * hits, axis=1)
-    slot = chosen * LANES + place
+    return (float_rows * lax.rsqrt(variance + 1e-06) * gain).astype(jnp.bfloat16)
 
-    count = experts * LANES
-    pick = (jnp.arange(count, dtype=jnp.int32)[:, None] == slot[None, :]).astype(jnp.bfloat16)
-    packed = jnp.dot(pick, normed, preferred_element_type=jnp.float32).astype(jnp.bfloat16)
-    back = experts_of(packed, gate_w, up_w, down_w)
-    combined = jnp.dot(pick.T, back, preferred_element_type=jnp.float32)
-    return (float_rows + scores * combined).astype(jnp.bfloat16)
+
+def first_kernel(rows_ref, gain_ref, chosen_ref, packed_ref, pick_ref):
+    count, rows = pick_ref.shape[1:]
+    earlier = lax.broadcasted_iota(jnp.int32, (rows, rows), 0) < lax.broadcasted_iota(
+        jnp.int32, (rows, rows), 1
+    )
+    earlier = earlier.astype(jnp.float32).astype(jnp.bfloat16)
+    lane = lax.broadcasted_iota(jnp.int32, (count, rows), 0)
+    for t in range(chosen_ref.shape[0]):
+        chosen = jnp.broadcast_to(chosen_ref[t : t + 1, :], (8, rows))
+        place = jnp.zeros((8, rows), jnp.float32)
+        for e in range(count // LANES):
+            mine = (chosen == e).astype(jnp.float32)
+            before = jnp.dot(
+                mine.astype(jnp.bfloat16), earlier, preferred_element_type=jnp.float32
+            )
+            place = place + mine * before
+        slot = chosen * LANES + place.astype(jnp.int32)
+        hit = lane == jnp.broadcast_to(slot[:1, :], (count, rows))
+        pick_ref[t] = hit.astype(jnp.float32).astype(jnp.bfloat16)
+    normed = normalise(rows_ref[...], gain_ref[...])
+    packed_ref[...] = jnp.dot(
+        pick_ref[0], normed, preferred_element_type=jnp.float32
+    ).astype(jnp.bfloat16)
+
+
+def first_step(rows, gain, chosen, count):
+    ticks, row_count = chosen.shape
+    width = rows.shape[1]
+    return pl.pallas_call(
+        first_kernel,
+        out_shape=[
+            jax.ShapeDtypeStruct((count, width), jnp.bfloat16),
+            jax.ShapeDtypeStruct((ticks, count, row_count), jnp.bfloat16),
+        ],
+        in_specs=[pl.BlockSpec(memory_space=pltpu.VMEM)] * 3,
+        out_specs=[pl.BlockSpec(memory_space=pltpu.VMEM)] * 2,
+        compiler_params=pltpu.CompilerParams(vmem_limit_bytes=16 * 2**20),
+    )(rows, gain, chosen)
 
 
 def local(pending, incoming, gain, gate_w, up_w, down_w, chosen, scores):
-    tick_total = chosen.shape[0]
+    ticks, row_count = chosen.shape[0], chosen.shape[2]
     first_section = lax.axis_index("pp") == 0
     count = lax.axis_size("pp")
     rows = pending[0]
+    packed, pick = first_step(
+        rows, gain, chosen.reshape(ticks, row_count), lax.axis_size("x") * LANES
+    )
     outputs = []
-    for tick in range(tick_total):
-        produced = section_layer(
-            rows, gain[0], gate_w[0], up_w[0], down_w[0], chosen[tick, 0], scores[tick, 0]
-        )
+    for tick in range(ticks):
+        if tick:
+            packed = select(pick[tick], normalise(rows, gain))
+        back = experts_of(packed, gate_w[0], up_w[0], down_w[0])
+        combined = jnp.dot(pick[tick].T, back, preferred_element_type=jnp.float32)
+        produced = (wide(rows) + scores[tick, 0] * combined).astype(jnp.bfloat16)
         outputs.append(produced)
-        if tick + 1 < tick_total:
+        if tick + 1 < ticks:
             passed = lax.ppermute(produced, "pp", [(i, i + 1) for i in range(count - 1)])
             rows = jnp.where(first_section, incoming[tick], passed)
     return jnp.stack(outputs)[:, None]

time: 296 us -> 294 us (level)
  other arithmetic: 10.1 us -> 6.94 us
where the time goes in v4:
time: 294 us; the launch traced here: 292 us
  blocking collectives  110 us (37%)
  starting transfers between devices  106 us (36%)
  waiting for transfers between devices  49 us (17%)
  Pallas kernels  10.9 us (4%)
  other arithmetic  6.94 us (2%)
  matrix products  4.98 us (2%)
  local copies, waits for them, and re-layouts  3.53 us (1%)
    ppermute x28, starting transfers between devices, shift(): lax.ppermute(value, 'y', [(i, (i + steps) % size) for i in range(size)])  95.9 us
    all_gather x2, blocking collectives, experts_of(): rows = lax.all_gather(mine.astype(jnp.float16), 'y', axis=0, tiled=True)  85.3 us
    all_to_all x2, blocking collectives, exchange(): moved = lax.all_to_all(blocks, 'x', split_axis=0, concat_axis=0, tiled=True)  24.7 us
    ppermute x28, waiting for transfers between devices, shift(): lax.ppermute(value, 'y', [(i, (i + steps) % size) for i in range(size)])  20.7 us
    all_to_all x2, waiting for transfers between devices, exchange(): moved = lax.all_to_all(blocks, 'x', split_axis=0, concat_axis=0, tiled=True)  20.2 us
    pallas_call x2, Pallas kernels, expert_parts(): pl.pallas_call(expert_kernel, out_shape=[pltpu.VMEM((total // GROUP, widt...  9.48 us
    all_to_all x2, starting transfers between devices, exchange(): moved = lax.all_to_all(blocks, 'x', split_axis=0, concat_axis=0, tiled=True)  8.6 us
    ppermute x1, waiting for transfers between devices, local(): lax.ppermute(produced, 'pp', [(i, i + 1) for i in range(count - 1)])  8.01 us
  transfers between devices with their start and end apart: 31, of which 7 were waited for; matrix products, arithmetic and copies ran while one was open for 1% of the time, Pallas kernels for 0%

profile of v4, /device:TPU:344, one launch (start us, length us, event | category | flops | bytes accessed | tf_op | source)
XLA Modules:
  0.0 292.3 jit_solution(17338509933046390817)
XLA Ops:
  8.1 11.2 %all-to-all-done = bf16[4,24,3584]{2,1,0:T(8,128)(2,1)S(1)} async-done(((bf16[4,24,3584]{2,1,0:T(8,128)(2,1)}), bf16[4,24,3584]{2,1,0:T(8,128)(2,1)S(1)}, u32[]{:S(2)}, u32[]{:S(2)}) %all-to-all-start) | async-done | bytes 688160 | tf_op jit(solution)/shard_map/all_to_all | solution.py:78
  19.7 43.6 %all-gather.2 = f16[576,3584]{1,0:T(8,128)(2,1)S(1)} all-gather(f16[72,3584]{1,0:T(8,128)(2,1)S(1)} %fusion.4), channel_id=1, replica_groups=mesh['pp'=16,'x'=4,'y'=8] {'y'}, dimensions={0}, use_global_device_ids=true | all-gather | bytes 4644864 | tf_op jit(solution)/shard_map/all_gather | solution.py:108
  65.1 4.7 %shard_map.83 = (bf16[72,1792]{1,0:T(8,128)(2,1)S(1)}, bf16[72,1792]{1,0:T(8,128)(2,1)S(1)}, bf16[72,1792]{1,0:T(8,128)(2,1)S(1)}, bf16[72,1792]{1,0:T(8,128)(2,...) custom-call(s32[1]{0:T(128)} %bitcast.4.me_ref, ...), custom_call_target="tpu_custom_call" | custom-call | flops 1585446912 | bytes 11010048 | tf_op jit(solution)/shard_map/pallas_call | solution.py:46
  81.8 5.1 %collective-permute-start.1 = (bf16[72,1792]{1,0:T(8,128)(2,1)S(1)}, bf16[72,1792]{1,0:T(8,128)(2,1)S(1)}, u32[]{:S(2)}, u32[]{:S(2)}) collective-permute-start(bf16[72,1792]{1,0:T(8,128)(2,1)S(1)} %add_convert_fusion.23), channel_id=1, source_target_pairs={{0,1},{1,2},{2,3},{3,4},{4,5},{5,6},{6,7},{7,0},{8,9},{9,10},{10,1... | collective-permute-start | bytes 774152 | tf_op jit(solution)/shard_map/ppermute | solution.py:15
  89.1 5.1 %collective-permute-start.8 = (bf16[72,1792]{1,0:T(8,128)(2,1)S(1)}, bf16[72,1792]{1,0:T(8,128)(2,1)S(1)}, u32[]{:S(2)}, u32[]{:S(2)}) collective-permute-start(bf16[72,1792]{1,0:T(8,128)(2,1)S(1)} %add_convert_fusion.17), channel_id=1, source_target_pairs={{0,1},{1,2},{2,3},{3,4},{4,5},{5,6},{6,7},{7,0},{8,9},{9,10},{10,1... | collective-permute-start | bytes 774152 | tf_op jit(solution)/shard_map/ppermute | solution.py:15
  96.3 5.1 %collective-permute-start.2 = (bf16[72,1792]{1,0:T(8,128)(2,1)S(1)}, bf16[72,1792]{1,0:T(8,128)(2,1)S(1)}, u32[]{:S(2)}, u32[]{:S(2)}) collective-permute-start(bf16[72,1792]{1,0:T(8,128)(2,1)S(1)} %add_convert_fusion.22), channel_id=1, source_target_pairs={{0,1},{1,2},{2,3},{3,4},{4,5},{5,6},{6,7},{7,0},{8,9},{9,10},{10,1... | collective-permute-start | bytes 774152 | tf_op jit(solution)/shard_map/ppermute | solution.py:15
  103.6 5.1 %collective-permute-start.9 = (bf16[72,1792]{1,0:T(8,128)(2,1)S(1)}, bf16[72,1792]{1,0:T(8,128)(2,1)S(1)}, u32[]{:S(2)}, u32[]{:S(2)}) collective-permute-start(bf16[72,1792]{1,0:T(8,128)(2,1)S(1)} %add_convert_fusion.16), channel_id=1, source_target_pairs={{0,1},{1,2},{2,3},{3,4},{4,5},{5,6},{6,7},{7,0},{8,9},{9,10},{10,1... | collective-permute-start | bytes 774152 | tf_op jit(solution)/shard_map/ppermute | solution.py:15
  110.8 5.1 %collective-permute-start.3 = (bf16[72,1792]{1,0:T(8,128)(2,1)S(1)}, bf16[72,1792]{1,0:T(8,128)(2,1)S(1)}, u32[]{:S(2)}, u32[]{:S(2)}) collective-permute-start(bf16[72,1792]{1,0:T(8,128)(2,1)S(1)} %add_convert_fusion.21), channel_id=1, source_target_pairs={{0,1},{1,2},{2,3},{3,4},{4,5},{5,6},{6,7},{7,0},{8,9},{9,10},{10,1... | collective-permute-start | bytes 774152 | tf_op jit(solution)/shard_map/ppermute | solution.py:15
  120.6 7.2 %collective-permute-done.13 = bf16[72,1792]{1,0:T(8,128)(2,1)S(1)} collective-permute-done((bf16[72,1792]{1,0:T(8,128)(2,1)S(1)}, bf16[72,1792]{1,0:T(8,128)(2,1)S(1)}, u32[]{:S(2)}, u32[]{:S(2)}) %collective-permute-start.13) | collective-permute-done | bytes 258080 | tf_op jit(solution)/shard_map/ppermute | solution.py:15
  129.0 4.3 %all-to-all-start.1 = ((bf16[4,24,3584]{2,1,0:T(8,128)(2,1)}), bf16[4,24,3584]{2,1,0:T(8,128)(2,1)}, u32[]{:S(2)}, u32[]{:S(2)}) async-start(bf16[4,24,3584]{2,1,0:T(8,128)(2,1)} %bitcast.50), calls=%async_computation.1 | async-start | bytes 1376256 | tf_op jit(solution)/shard_map/all_to_all | solution.py:78
  133.3 9.0 %all-to-all-done.1 = bf16[4,24,3584]{2,1,0:T(8,128)(2,1)} async-done(((bf16[4,24,3584]{2,1,0:T(8,128)(2,1)}), bf16[4,24,3584]{2,1,0:T(8,128)(2,1)}, u32[]{:S(2)}, u32[]{:S(2)}) %all-to-all-start.1) | async-done | bytes 688160 | tf_op jit(solution)/shard_map/all_to_all | solution.py:78
  146.5 8.0 %collective-permute-done.14 = bf16[64,3584]{1,0:T(8,128)(2,1)S(1)} collective-permute-done((bf16[64,3584]{1,0:T(8,128)(2,1)}, bf16[64,3584]{1,0:T(8,128)(2,1)S(1)}, u32[]{:S(2)}, u32[]{:S(2)}) %collective-permute-start.14) | collective-permute-done | bytes 458784 | tf_op jit(solution)/shard_map/ppermute | solution.py:177
  156.2 13.3 %all_to_all.20 = bf16[4,24,3584]{2,1,0:T(8,128)(2,1)S(1)} all-to-all(bf16[4,24,3584]{2,1,0:T(8,128)(2,1)S(1)} %bitcast.52), channel_id=1, replica_groups=mesh['pp'=16,'x'=4,'y'=8] {'x'}, dimensions={0} | all-to-all | bytes 1376256 | tf_op jit(solution)/shard_map/all_to_all | solution.py:78
  169.9 41.7 %all-gather.3 = f16[576,3584]{1,0:T(8,128)(2,1)S(1)} all-gather(f16[72,3584]{1,0:T(8,128)(2,1)S(1)} %fusion.5), channel_id=1, replica_groups=mesh['pp'=16,'x'=4,'y'=8] {'y'}, dimensions={0}, use_global_device_ids=true | all-gather | bytes 4644864 | tf_op jit(solution)/shard_map/all_gather | solution.py:108
  212.2 4.7 %shard_map.84 = (bf16[72,1792]{1,0:T(8,128)(2,1)S(1)}, bf16[72,1792]{1,0:T(8,128)(2,1)S(1)}, bf16[72,1792]{1,0:T(8,128)(2,1)S(1)}, bf16[72,1792]{1,0:T(8,128)(2,...) custom-call(s32[1]{0:T(128)} %bitcast.4.me_ref, ...), custom_call_target="tpu_custom_call" | custom-call | flops 1585446912 | bytes 11010048 | tf_op jit(solution)/shard_map/pallas_call | solution.py:46
  217.0 4.5 %collective-permute-start.15 = (bf16[72,1792]{1,0:T(8,128)(2,1)S(1)}, bf16[72,1792]{1,0:T(8,128)(2,1)S(1)}, u32[]{:S(2)}, u32[]{:S(2)}) collective-permute-start(bf16[72,1792]{1,0:T(8,128)(2,1)S(1)} %get-tuple-element.58), channel_id=1, source_target_pairs={{0,1},{1,2},{2,3},{3,4},{4,5},{5,6},{6,7},{7,0},{8,9},{9,10},{10,1... | collective-permute-start | bytes 774152 | tf_op jit(solution)/shard_map/ppermute | solution.py:15
  223.4 5.1 %collective-permute-start.22 = (bf16[72,1792]{1,0:T(8,128)(2,1)S(1)}, bf16[72,1792]{1,0:T(8,128)(2,1)S(1)}, u32[]{:S(2)}, u32[]{:S(2)}) collective-permute-start(bf16[72,1792]{1,0:T(8,128)(2,1)S(1)} %get-tuple-element.66), channel_id=1, source_target_pairs={{0,1},{1,2},{2,3},{3,4},{4,5},{5,6},{6,7},{7,0},{8,9},{9,10},{10,1... | collective-permute-start | bytes 774152 | tf_op jit(solution)/shard_map/ppermute | solution.py:15
  230.5 5.1 %collective-permute-start.16 = (bf16[72,1792]{1,0:T(8,128)(2,1)S(1)}, bf16[72,1792]{1,0:T(8,128)(2,1)S(1)}, u32[]{:S(2)}, u32[]{:S(2)}) collective-permute-start(bf16[72,1792]{1,0:T(8,128)(2,1)S(1)} %add_convert_fusion.11), channel_id=1, source_target_pairs={{0,1},{1,2},{2,3},{3,4},{4,5},{5,6},{6,7},{7,0},{8,9},{9,10},{10,1... | collective-permute-start | bytes 774152 | tf_op jit(solution)/shard_map/ppermute | solution.py:15
  237.8 5.1 %collective-permute-start.23 = (bf16[72,1792]{1,0:T(8,128)(2,1)S(1)}, bf16[72,1792]{1,0:T(8,128)(2,1)S(1)}, u32[]{:S(2)}, u32[]{:S(2)}) collective-permute-start(bf16[72,1792]{1,0:T(8,128)(2,1)S(1)} %add_convert_fusion.5), channel_id=1, source_target_pairs={{0,1},{1,2},{2,3},{3,4},{4,5},{5,6},{6,7},{7,0},{8,9},{9,10},{10,1... | collective-permute-start | bytes 774152 | tf_op jit(solution)/shard_map/ppermute | solution.py:15
  245.0 5.1 %collective-permute-start.17 = (bf16[72,1792]{1,0:T(8,128)(2,1)S(1)}, bf16[72,1792]{1,0:T(8,128)(2,1)S(1)}, u32[]{:S(2)}, u32[]{:S(2)}) collective-permute-start(bf16[72,1792]{1,0:T(8,128)(2,1)S(1)} %add_convert_fusion.10), channel_id=1, source_target_pairs={{0,1},{1,2},{2,3},{3,4},{4,5},{5,6},{6,7},{7,0},{8,9},{9,10},{10,1... | collective-permute-start | bytes 774152 | tf_op jit(solution)/shard_map/ppermute | solution.py:15
  252.2 5.1 %collective-permute-start.24 = (bf16[72,1792]{1,0:T(8,128)(2,1)S(1)}, bf16[72,1792]{1,0:T(8,128)(2,1)S(1)}, u32[]{:S(2)}, u32[]{:S(2)}) collective-permute-start(bf16[72,1792]{1,0:T(8,128)(2,1)S(1)} %add_convert_fusion.4), channel_id=1, source_target_pairs={{0,1},{1,2},{2,3},{3,4},{4,5},{5,6},{6,7},{7,0},{8,9},{9,10},{10,1... | collective-permute-start | bytes 774152 | tf_op jit(solution)/shard_map/ppermute | solution.py:15
  259.5 5.1 %collective-permute-start.18 = (bf16[72,1792]{1,0:T(8,128)(2,1)S(1)}, bf16[72,1792]{1,0:T(8,128)(2,1)S(1)}, u32[]{:S(2)}, u32[]{:S(2)}) collective-permute-start(bf16[72,1792]{1,0:T(8,128)(2,1)S(1)} %add_convert_fusion.9), channel_id=1, source_target_pairs={{0,1},{1,2},{2,3},{3,4},{4,5},{5,6},{6,7},{7,0},{8,9},{9,10},{10,1... | collective-permute-start | bytes 774152 | tf_op jit(solution)/shard_map/ppermute | solution.py:15
  271.0 7.2 %collective-permute-done.28 = bf16[72,1792]{1,0:T(8,128)(2,1)S(1)} collective-permute-done((bf16[72,1792]{1,0:T(8,128)(2,1)S(1)}, bf16[72,1792]{1,0:T(8,128)(2,1)S(1)}, u32[]{:S(2)}, u32[]{:S(2)}) %collective-permute-start.28) | collective-permute-done | bytes 258080 | tf_op jit(solution)/shard_map/ppermute | solution.py:15
  278.5 11.4 %all_to_all.21 = bf16[4,24,3584]{2,1,0:T(8,128)(2,1)S(1)} all-to-all(bf16[4,24,3584]{2,1,0:T(8,128)(2,1)S(1)} %bitcast.53), channel_id=1, replica_groups=mesh['pp'=16,'x'=4,'y'=8] {'x'}, dimensions={0} | all-to-all | bytes 1376256 | tf_op jit(solution)/shard_map/all_to_all | solution.py:78
  (102 shorter events, 64.4 us)
Async XLA Ops:
  3.8 15.5 %all-to-all-start = ((bf16[4,24,3584]{2,1,0:T(8,128)(2,1)}), bf16[4,24,3584]{2,1,0:T(8,128)(2,1)S(1)}, u32[]{:S(2)}, u32[]{:S(2)}) async-start(bf16[4,24,3584]{2,1,0:T(8,128)(2,1)} %bitcast.5), calls=%async_computation | async-start | bytes 1376256 | tf_op jit(solution)/shard_map/all_to_all | solution.py:78
  69.8 12.0 %collective-permute-start = (bf16[72,1792]{1,0:T(8,128)(2,1)S(1)}, bf16[72,1792]{1,0:T(8,128)(2,1)S(1)}, u32[]{:S(2)}, u32[]{:S(2)}) collective-permute-start(bf16[72,1792]{1,0:T(8,128)(2,1)S(1)} %get-tuple-element.42), channel_id=1, source_target_pairs={{0,1},{1,2},{2,3},{3,4},{4,5},{5,6},{6,7},{7,0},{8,9},{9,10},{10,1... | collective-permute-start | bytes 774152 | tf_op jit(solution)/shard_map/ppermute | solution.py:15
  72.8 14.2 %collective-permute-start.4 = (bf16[72,1792]{1,0:T(8,128)(2,1)S(1)}, bf16[72,1792]{1,0:T(8,128)(2,1)S(1)}, u32[]{:S(2)}, u32[]{:S(2)}) collective-permute-start(bf16[72,1792]{1,0:T(8,128)(2,1)S(1)} %get-tuple-element.46), channel_id=1, source_target_pairs={{0,7},{1,0},{2,1},{3,2},{4,3},{5,4},{6,5},{7,6},{8,15},{9,8},{10,9... | collective-permute-start | bytes 774152 | tf_op jit(solution)/shard_map/ppermute | solution.py:15
  75.7 13.3 %collective-permute-start.7 = (bf16[72,1792]{1,0:T(8,128)(2,1)S(1)}, bf16[72,1792]{1,0:T(8,128)(2,1)S(1)}, u32[]{:S(2)}, u32[]{:S(2)}) collective-permute-start(bf16[72,1792]{1,0:T(8,128)(2,1)S(1)} %get-tuple-element.50), channel_id=1, source_target_pairs={{0,1},{1,2},{2,3},{3,4},{4,5},{5,6},{6,7},{7,0},{8,9},{9,10},{10,1... | collective-permute-start | bytes 774152 | tf_op jit(solution)/shard_map/ppermute | solution.py:15
  79.8 14.4 %collective-permute-start.10 = (bf16[72,1792]{1,0:T(8,128)(2,1)S(1)}, bf16[72,1792]{1,0:T(8,128)(2,1)S(1)}, u32[]{:S(2)}, u32[]{:S(2)}) collective-permute-start(bf16[72,1792]{1,0:T(8,128)(2,1)S(1)} %get-tuple-element.53), channel_id=1, source_target_pairs={{0,7},{1,0},{2,1},{3,2},{4,3},{5,4},{6,5},{7,6},{8,15},{9,8},{10,9... | collective-permute-start | bytes 774152 | tf_op jit(solution)/shard_map/ppermute | solution.py:15
  81.8 14.4 %collective-permute-start.1 = (bf16[72,1792]{1,0:T(8,128)(2,1)S(1)}, bf16[72,1792]{1,0:T(8,128)(2,1)S(1)}, u32[]{:S(2)}, u32[]{:S(2)}) collective-permute-start(bf16[72,1792]{1,0:T(8,128)(2,1)S(1)} %add_convert_fusion.23), channel_id=1, source_target_pairs={{0,1},{1,2},{2,3},{3,4},{4,5},{5,6},{6,7},{7,0},{8,9},{9,10},{10,1... | collective-permute-start | bytes 774152 | tf_op jit(solution)/shard_map/ppermute | solution.py:15
  87.1 14.4 %collective-permute-start.5 = (bf16[72,1792]{1,0:T(8,128)(2,1)S(1)}, bf16[72,1792]{1,0:T(8,128)(2,1)S(1)}, u32[]{:S(2)}, u32[]{:S(2)}) collective-permute-start(bf16[72,1792]{1,0:T(8,128)(2,1)S(1)} %add_convert_fusion.20), channel_id=1, source_target_pairs={{0,7},{1,0},{2,1},{3,2},{4,3},{5,4},{6,5},{7,6},{8,15},{9,8},{10,9... | collective-permute-start | bytes 774152 | tf_op jit(solution)/shard_map/ppermute | solution.py:15
  89.1 14.4 %collective-permute-start.8 = (bf16[72,1792]{1,0:T(8,128)(2,1)S(1)}, bf16[72,1792]{1,0:T(8,128)(2,1)S(1)}, u32[]{:S(2)}, u32[]{:S(2)}) collective-permute-start(bf16[72,1792]{1,0:T(8,128)(2,1)S(1)} %add_convert_fusion.17), channel_id=1, source_target_pairs={{0,1},{1,2},{2,3},{3,4},{4,5},{5,6},{6,7},{7,0},{8,9},{9,10},{10,1... | collective-permute-start | bytes 774152 | tf_op jit(solution)/shard_map/ppermute | solution.py:15
  94.3 14.4 %collective-permute-start.11 = (bf16[72,1792]{1,0:T(8,128)(2,1)S(1)}, bf16[72,1792]{1,0:T(8,128)(2,1)S(1)}, u32[]{:S(2)}, u32[]{:S(2)}) collective-permute-start(bf16[72,1792]{1,0:T(8,128)(2,1)S(1)} %add_convert_fusion.15), channel_id=1, source_target_pairs={{0,7},{1,0},{2,1},{3,2},{4,3},{5,4},{6,5},{7,6},{8,15},{9,8},{10,9... | collective-permute-start | bytes 774152 | tf_op jit(solution)/shard_map/ppermute | solution.py:15
  96.3 14.4 %collective-permute-start.2 = (bf16[72,1792]{1,0:T(8,128)(2,1)S(1)}, bf16[72,1792]{1,0:T(8,128)(2,1)S(1)}, u32[]{:S(2)}, u32[]{:S(2)}) collective-permute-start(bf16[72,1792]{1,0:T(8,128)(2,1)S(1)} %add_convert_fusion.22), channel_id=1, source_target_pairs={{0,1},{1,2},{2,3},{3,4},{4,5},{5,6},{6,7},{7,0},{8,9},{9,10},{10,1... | collective-permute-start | bytes 774152 | tf_op jit(solution)/shard_map/ppermute | solution.py:15
  101.5 18.7 %collective-permute-start.6 = (bf16[72,1792]{1,0:T(8,128)(2,1)S(1)}, bf16[72,1792]{1,0:T(8,128)(2,1)S(1)}, u32[]{:S(2)}, u32[]{:S(2)}) collective-permute-start(bf16[72,1792]{1,0:T(8,128)(2,1)S(1)} %add_convert_fusion.19), channel_id=1, source_target_pairs={{0,7},{1,0},{2,1},{3,2},{4,3},{5,4},{6,5},{7,6},{8,15},{9,8},{10,9... | collective-permute-start | bytes 774152 | tf_op jit(solution)/shard_map/ppermute | solution.py:15
  103.6 17.0 %collective-permute-start.9 = (bf16[72,1792]{1,0:T(8,128)(2,1)S(1)}, bf16[72,1792]{1,0:T(8,128)(2,1)S(1)}, u32[]{:S(2)}, u32[]{:S(2)}) collective-permute-start(bf16[72,1792]{1,0:T(8,128)(2,1)S(1)} %add_convert_fusion.16), channel_id=1, source_target_pairs={{0,1},{1,2},{2,3},{3,4},{4,5},{5,6},{6,7},{7,0},{8,9},{9,10},{10,1... | collective-permute-start | bytes 774152 | tf_op jit(solution)/shard_map/ppermute | solution.py:15
  129.0 13.3 %all-to-all-start.1 = ((bf16[4,24,3584]{2,1,0:T(8,128)(2,1)}), bf16[4,24,3584]{2,1,0:T(8,128)(2,1)}, u32[]{:S(2)}, u32[]{:S(2)}) async-start(bf16[4,24,3584]{2,1,0:T(8,128)(2,1)} %bitcast.50), calls=%async_computation.1 | async-start | bytes 1376256 | tf_op jit(solution)/shard_map/all_to_all | solution.py:78
  217.0 13.5 %collective-permute-start.15 = (bf16[72,1792]{1,0:T(8,128)(2,1)S(1)}, bf16[72,1792]{1,0:T(8,128)(2,1)S(1)}, u32[]{:S(2)}, u32[]{:S(2)}) collective-permute-start(bf16[72,1792]{1,0:T(8,128)(2,1)S(1)} %get-tuple-element.58), channel_id=1, source_target_pairs={{0,1},{1,2},{2,3},{3,4},{4,5},{5,6},{6,7},{7,0},{8,9},{9,10},{10,1... | collective-permute-start | bytes 774152 | tf_op jit(solution)/shard_map/ppermute | solution.py:15
  221.4 14.2 %collective-permute-start.19 = (bf16[72,1792]{1,0:T(8,128)(2,1)S(1)}, bf16[72,1792]{1,0:T(8,128)(2,1)S(1)}, u32[]{:S(2)}, u32[]{:S(2)}) collective-permute-start(bf16[72,1792]{1,0:T(8,128)(2,1)S(1)} %get-tuple-element.62), channel_id=1, source_target_pairs={{0,7},{1,0},{2,1},{3,2},{4,3},{5,4},{6,5},{7,6},{8,15},{9,8},{10,9... | collective-permute-start | bytes 774152 | tf_op jit(solution)/shard_map/ppermute | solution.py:15
  223.4 14.3 %collective-permute-start.22 = (bf16[72,1792]{1,0:T(8,128)(2,1)S(1)}, bf16[72,1792]{1,0:T(8,128)(2,1)S(1)}, u32[]{:S(2)}, u32[]{:S(2)}) collective-permute-start(bf16[72,1792]{1,0:T(8,128)(2,1)S(1)} %get-tuple-element.66), channel_id=1, source_target_pairs={{0,1},{1,2},{2,3},{3,4},{4,5},{5,6},{6,7},{7,0},{8,9},{9,10},{10,1... | collective-permute-start | bytes 774152 | tf_op jit(solution)/shard_map/ppermute | solution.py:15
  228.5 14.4 %collective-permute-start.25 = (bf16[72,1792]{1,0:T(8,128)(2,1)S(1)}, bf16[72,1792]{1,0:T(8,128)(2,1)S(1)}, u32[]{:S(2)}, u32[]{:S(2)}) collective-permute-start(bf16[72,1792]{1,0:T(8,128)(2,1)S(1)} %get-tuple-element.69), channel_id=1, source_target_pairs={{0,7},{1,0},{2,1},{3,2},{4,3},{5,4},{6,5},{7,6},{8,15},{9,8},{10,9... | collective-permute-start | bytes 774152 | tf_op jit(solution)/shard_map/ppermute | solution.py:15
  230.5 14.4 %collective-permute-start.16 = (bf16[72,1792]{1,0:T(8,128)(2,1)S(1)}, bf16[72,1792]{1,0:T(8,128)(2,1)S(1)}, u32[]{:S(2)}, u32[]{:S(2)}) collective-permute-start(bf16[72,1792]{1,0:T(8,128)(2,1)S(1)} %add_convert_fusion.11), channel_id=1, source_target_pairs={{0,1},{1,2},{2,3},{3,4},{4,5},{5,6},{6,7},{7,0},{8,9},{9,10},{10,1... | collective-permute-start | bytes 774152 | tf_op jit(solution)/shard_map/ppermute | solution.py:15
  235.7 14.4 %collective-permute-start.20 = (bf16[72,1792]{1,0:T(8,128)(2,1)S(1)}, bf16[72,1792]{1,0:T(8,128)(2,1)S(1)}, u32[]{:S(2)}, u32[]{:S(2)}) collective-permute-start(bf16[72,1792]{1,0:T(8,128)(2,1)S(1)} %add_convert_fusion.8), channel_id=1, source_target_pairs={{0,7},{1,0},{2,1},{3,2},{4,3},{5,4},{6,5},{7,6},{8,15},{9,8},{10,9... | collective-permute-start | bytes 774152 | tf_op jit(solution)/shard_map/ppermute | solution.py:15
  237.8 14.4 %collective-permute-start.23 = (bf16[72,1792]{1,0:T(8,128)(2,1)S(1)}, bf16[72,1792]{1,0:T(8,128)(2,1)S(1)}, u32[]{:S(2)}, u32[]{:S(2)}) collective-permute-start(bf16[72,1792]{1,0:T(8,128)(2,1)S(1)} %add_convert_fusion.5), channel_id=1, source_target_pairs={{0,1},{1,2},{2,3},{3,4},{4,5},{5,6},{6,7},{7,0},{8,9},{9,10},{10,1... | collective-permute-start | bytes 774152 | tf_op jit(solution)/shard_map/ppermute | solution.py:15
  243.0 14.4 %collective-permute-start.26 = (bf16[72,1792]{1,0:T(8,128)(2,1)S(1)}, bf16[72,1792]{1,0:T(8,128)(2,1)S(1)}, u32[]{:S(2)}, u32[]{:S(2)}) collective-permute-start(bf16[72,1792]{1,0:T(8,128)(2,1)S(1)} %add_convert_fusion.3), channel_id=1, source_target_pairs={{0,7},{1,0},{2,1},{3,2},{4,3},{5,4},{6,5},{7,6},{8,15},{9,8},{10,9... | collective-permute-start | bytes 774152 | tf_op jit(solution)/shard_map/ppermute | solution.py:15
  245.0 14.4 %collective-permute-start.17 = (bf16[72,1792]{1,0:T(8,128)(2,1)S(1)}, bf16[72,1792]{1,0:T(8,128)(2,1)S(1)}, u32[]{:S(2)}, u32[]{:S(2)}) collective-permute-start(bf16[72,1792]{1,0:T(8,128)(2,1)S(1)} %add_convert_fusion.10), channel_id=1, source_target_pairs={{0,1},{1,2},{2,3},{3,4},{4,5},{5,6},{6,7},{7,0},{8,9},{9,10},{10,1... | collective-permute-start | bytes 774152 | tf_op jit(solution)/shard_map/ppermute | solution.py:15
  250.2 20.4 %collective-permute-start.21 = (bf16[72,1792]{1,0:T(8,128)(2,1)S(1)}, bf16[72,1792]{1,0:T(8,128)(2,1)S(1)}, u32[]{:S(2)}, u32[]{:S(2)}) collective-permute-start(bf16[72,1792]{1,0:T(8,128)(2,1)S(1)} %add_convert_fusion.7), channel_id=1, source_target_pairs={{0,7},{1,0},{2,1},{3,2},{4,3},{5,4},{6,5},{7,6},{8,15},{9,8},{10,9... | collective-permute-start | bytes 774152 | tf_op jit(solution)/shard_map/ppermute | solution.py:15
  252.2 18.8 %collective-permute-start.24 = (bf16[72,1792]{1,0:T(8,128)(2,1)S(1)}, bf16[72,1792]{1,0:T(8,128)(2,1)S(1)}, u32[]{:S(2)}, u32[]{:S(2)}) collective-permute-start(bf16[72,1792]{1,0:T(8,128)(2,1)S(1)} %add_convert_fusion.4), channel_id=1, source_target_pairs={{0,1},{1,2},{2,3},{3,4},{4,5},{5,6},{6,7},{7,0},{8,9},{9,10},{10,1... | collective-permute-start | bytes 774152 | tf_op jit(solution)/shard_map/ppermute | solution.py:15
  (16 other events, 113.9 us)
